TPU v7x, 32 devices: a whole 2x2x4 slice. The times are simulated.
32 devices in a mesh: shard: 8 (over z, x), blk: 4 (over y, core).
Axes of the slice: x: 2, y: 2, z: 4, core: 2. Of those that a mesh axis runs over, the one named last changes fastest.
Arguments:
- query_vectors: bfloat16 [8192, 256], P(('shard', 'blk')), may hold values from -6 to 6
- holding_devices: int32 [8192, 4], P(('shard', 'blk')), may hold values from 0 to 31, all different within a row; in each aligned block of 256 rows (0 to 255, 256 to 511, ...) at most 64 rows name the same one
- local_slot_number: int32 [8192, 4], P(('shard', 'blk')), may hold values from 0 to 4095
- valid_item_tally: int32 [8192], P(('shard', 'blk')), may hold values from 1 to 4
- score_stretch: float32 [1], replicated, may hold values from 1 to 4
- offset_term: float32 [1], replicated, may hold values from -4 to -1
- item_embedding_matrix: float32 [131072, 256], P(('shard', 'blk')), may hold values from -0.5 to 0.5
- running_grad_energy: float32 [131072, 256], P(('shard', 'blk')), may hold values from 1e-05 to 0.001
Outputs:
- table_out: float32 [131072, 256], P(('shard', 'blk'))
- new_square_sums: float32 [131072, 256], P(('shard', 'blk'))
Inputs may be any that keep to these rules, and one draw needn't show every extreme that they name: `holding_devices`: the 4 owners listed for one example are distinct. Among the 256 examples of one device at most 64 ids name one owner, and this bound is reached.
All inputs are finite; a program needn't handle non-finite values.
Results may differ from a plain program's by a relative error of at most 0.014.
Values may be sent and summed in bfloat16 or wider, within the bound.
No kernel may reach another device: no remote copies, remote signals or barrier semaphores. Data moves between devices by JAX's collectives and lax.ppermute only.
A program may use at most 64 MiB of HBM per device.

v0:
```python
import jax
import jax.numpy as jnp
from jax import lax
from jax.sharding import PartitionSpec as P

LEARN_RATE = 0.5
ADAGRAD_EPSILON = 1e-08


def per_device(
    query_vectors,
    holding_devices,
    local_slot_number,
    valid_item_tally,
    score_stretch,
    offset_term,
    item_embedding_matrix,
    running_grad_energy,
):
    examples, bag_size = holding_devices.shape
    feature_width = item_embedding_matrix.shape[1]
    devices = lax.axis_size(("shard", "blk"))
    blocks = lax.axis_size("blk")
    capacity = max(2, 2 * examples * bag_size // devices)
    group_size = examples * blocks
    score_multiplier = score_stretch[0]
    offset = offset_term[0]
    flat_owner_index = holding_devices.reshape(-1)
    local_flat = local_slot_number.reshape(-1)
    onehot = (flat_owner_index[:, None] == jnp.arange(devices, dtype=jnp.int32)[None, :]).astype(
        jnp.int32
    )
    slot_rank = jnp.sum((jnp.cumsum(onehot, axis=0) - 1) * onehot, axis=1)
    slot_index = flat_owner_index * capacity + slot_rank
    requests = jnp.zeros((devices * capacity,), jnp.int32).at[slot_index].set(local_flat)
    requests = requests.reshape(devices, capacity)
    wanted = lax.all_to_all(requests, ("shard", "blk"), split_axis=0, concat_axis=0, tiled=True)
    fetched_rows = item_embedding_matrix[wanted].astype(jnp.bfloat16)
    answered = lax.all_to_all(
        fetched_rows, ("shard", "blk"), split_axis=0, concat_axis=0, tiled=True
    )
    slot_rows = answered.reshape(devices * capacity, feature_width)[slot_index]
    slot_rows = slot_rows.reshape(examples, bag_size, feature_width)
    positions = jnp.arange(bag_size, dtype=jnp.int32)
    in_bag = positions[None, :] < valid_item_tally[:, None]
    weight = jnp.where(in_bag, 1.0, 0.0).astype(jnp.float32) / valid_item_tally[:, None].astype(
        jnp.float32
    )
    item_vecs = jnp.sum(slot_rows.astype(jnp.float32) * weight[:, :, None], axis=1).astype(
        jnp.bfloat16
    )
    own_start = lax.axis_index("blk") * examples
    own_rows = own_start + jnp.arange(examples, dtype=jnp.int32)
    shard_piece = lax.all_gather(item_vecs, "blk", axis=0, tiled=True)
    scores = (
        score_multiplier * jnp.dot(query_vectors, shard_piece.T, preferred_element_type=jnp.float32)
        + offset
    )
    others = jnp.arange(shard_piece.shape[0], dtype=jnp.int32)
    labels = jnp.where(own_rows[:, None] == others[None, :], 1.0, -1.0).astype(jnp.float32)
    coef = (
        labels * (jax.nn.sigmoid(labels * scores) - 1.0) * score_multiplier / group_size
    ).astype(jnp.bfloat16)
    item_grad = lax.psum_scatter(
        lax.dot_general(
            coef, query_vectors, (((0,), (0,)), ((), ())), preferred_element_type=jnp.float32
        ).astype(jnp.bfloat16),
        "blk",
        scatter_dimension=0,
        tiled=True,
    ).astype(jnp.float32)
    slot_grad = (item_grad[:, None, :] * weight[:, :, None]).reshape(
        examples * bag_size, feature_width
    )
    outgoing = (
        jnp.zeros((devices * capacity, feature_width), jnp.float32).at[slot_index].set(slot_grad)
    )
    outgoing = outgoing.reshape(devices, capacity, feature_width)
    incoming = lax.all_to_all(
        outgoing.astype(jnp.bfloat16), ("shard", "blk"), split_axis=0, concat_axis=0, tiled=True
    ).astype(outgoing.dtype)
    row_gradient = (
        jnp.zeros_like(item_embedding_matrix)
        .at[wanted.reshape(-1)]
        .add(incoming.reshape(devices * capacity, feature_width))
    )
    new_square_sums = running_grad_energy + row_gradient * row_gradient
    table_out = item_embedding_matrix - LEARN_RATE * row_gradient / (
        jnp.sqrt(new_square_sums) + ADAGRAD_EPSILON
    )
    return (table_out, new_square_sums)


def solution(mesh):
    placed = (
        P(("shard", "blk"), None),
        P(("shard", "blk"), None),
        P(("shard", "blk"), None),
        P(("shard", "blk")),
        P(),
        P(),
        P(("shard", "blk"), None),
        P(("shard", "blk"), None),
    )
    return jax.shard_map(
        per_device,
        mesh=mesh,
        in_specs=placed,
        out_specs=(P(("shard", "blk"), None), P(("shard", "blk"), None)),
        check_vma=False,
    )
```

profile of v0, /device:TPU:0, one launch (start us, length us, event | category | flops | bytes accessed | tf_op | source)
XLA Modules:
  0.0 182.7 jit_solution(12576803808827260025)
XLA Ops:
  7.2 0.7 broadcast_multiply_fusion
  7.9 0.8 copy.11
  9.3 9.0 %reduce-window.6 = s32[32,8,128]{2,1,0:T(8,128)S(1)} reduce-window(s32[32,8,128]{2,1,0:T(8,128)S(1)} %fusion.26, s32[]{:T(128)} %constant.14.clone.1), window={size=1x1x128 pad=0_0x0_0x127_0}, to_apply=%region_0.0 | reduce-window | flops 4161536 | bytes 262148 | tf_op jit(solution)/shard_map/reduce-window
  18.7 0.8 copy.15
  19.7 4.3 %scatter_custom_fusion = s32[2048]{0:T(1024)S(1)} fusion(s32[1024]{0:T(1024)S(1)} %bitcast.64, s32[1024]{0:T(1024)S(1)} %reshape.218, s32[]{:T(128)} %constant.14.clone.1), kind=kCustom, calls=%fused_computation.50 | custom fusion | bytes 8196 | tf_op jit(solution)/shard_map/scatter | solution.py:35
  24.1 14.3 %all_to_all.22 = s32[32,1,64]{2,1,0:T(1,128)S(1)} all-to-all(s32[32,1,64]{2,1,0:T(1,128)S(1)} %all_to_all.14), channel_id=1, replica_groups=mesh['shard'=8,'blk'=4] {'shard','blk'}, dimensions={0} | all-to-all | bytes 16384 | tf_op jit(solution)/shard_map/all_to_all | solution.py:37
  38.5 10.7 %gather_fusion = bf16[2048,256]{1,0:T(8,128)(2,1)} fusion(f32[4096,256]{1,0:T(8,128)} %param.14, s32[2048]{0:T(1024)S(1)} %broadcast_clamp_fusion), kind=kCustom, calls=%fused_computation | custom fusion | bytes 2105344 | tf_op jit(solution)/shard_map/gather | solution.py:38
  49.2 2.6 %all-to-all-start.1 = ((bf16[32,64,256]{2,1,0:T(8,128)(2,1)}), bf16[32,64,256]{2,1,0:T(8,128)(2,1)S(1)}, u32[]{:S(2)}, u32[]{:S(2)}) async-start(bf16[32,64,256]{2,1,0:T(8,128)(2,1)} %bitcast.7), calls=%async_computation.1 | async-start | bytes 2097152 | tf_op jit(solution)/shard_map/all_to_all | solution.py:39
  53.4 24.7 %all-to-all-done.1 = bf16[32,64,256]{2,1,0:T(8,128)(2,1)S(1)} async-done(((bf16[32,64,256]{2,1,0:T(8,128)(2,1)}), bf16[32,64,256]{2,1,0:T(8,128)(2,1)S(1)}, u32[]{:S(2)}, u32[]{:S(2)}) %all-to-all-start.1) | async-done | bytes 1048608 | tf_op jit(solution)/shard_map/all_to_all | solution.py:39
  78.1 3.9 %gather_fusion.1 = bf16[1024,256]{1,0:T(8,128)(2,1)S(1)} fusion(bf16[2048,256]{1,0:T(8,128)(2,1)S(1)} %bitcast.58, s32[1024]{0:T(1024)S(1)} %broadcast_clamp_fusion.1), kind=kCustom, calls=%fused_computation.1 | custom fusion | bytes 1052672 | tf_op jit(solution)/shard_map/gather | solution.py:42
  82.3 0.7 multiply_reduce_fusion
  83.0 7.2 %all_gather.3 = bf16[1024,256]{1,0:T(8,128)(2,1)S(1)} all-gather(bf16[256,256]{1,0:T(8,128)(2,1)S(1)} %multiply_reduce_fusion), channel_id=1, replica_groups=mesh['shard'=8,'blk'=4] {'blk'}, dimensions={0}, use_global_device_ids=true | all-gather | bytes 655360 | tf_op jit(solution)/shard_map/all_gather | solution.py:54
  90.2 1.8 convolution_convert_fusion
  92.1 20.5 %reduce-scatter.2.cloned.1.call-done = bf16[256,256]{1,0:T(8,128)(2,1)} async-done(((bf16[1024,256]{1,0:T(8,128)(2,1)}), bf16[256,256]{1,0:T(8,128)(2,1)}) %reduce-scatter.2.cloned.1.call-update) | async-done | bytes 131088 | tf_op jit(solution)/shard_map/reduce_scatter | solution.py:64
  112.6 1.0 mul.87
  113.6 0.4 mul.88
  114.0 5.8 %scatter_custom_fusion.1 = f32[2048,256]{1,0:T(8,128)S(1)} fusion(s32[1024]{0:T(1024)S(1)} %bitcast.66, f32[1024,256]{1,0:T(8,128)S(1)} %mul.88, f32[]{:T(128)} %constant.13.clone.1, f32[1024]{0:T(1024)S(1)} %div.33), kind=kCustom, calls=%fused_computation.24 | custom fusion | flops 262144 | bytes 3149828 | tf_op jit(solution)/shard_map/scatter | solution.py:76
  119.8 1.1 convert_element_type.46
  120.9 4.6 %all-to-all-start.2 = ((bf16[32,64,256]{2,1,0:T(8,128)(2,1)}), bf16[32,64,256]{2,1,0:T(8,128)(2,1)S(1)}, u32[]{:S(2)}, u32[]{:S(2)}) async-start(bf16[32,64,256]{2,1,0:T(8,128)(2,1)} %bitcast.11), calls=%async_computation.3 | async-start | bytes 2097152 | tf_op jit(solution)/shard_map/all_to_all | solution.py:79
  125.5 0.5 broadcast.165
  126.0 0.7 reduce.3
  126.8 24.9 %all-to-all-done.2 = bf16[32,64,256]{2,1,0:T(8,128)(2,1)S(1)} async-done(((bf16[32,64,256]{2,1,0:T(8,128)(2,1)}), bf16[32,64,256]{2,1,0:T(8,128)(2,1)S(1)}, u32[]{:S(2)}, u32[]{:S(2)}) %all-to-all-start.2) | async-done | bytes 1048608 | tf_op jit(solution)/shard_map/all_to_all | solution.py:79
  151.7 14.3 %scatter_custom_fusion.2 = f32[4096,256]{1,0:T(8,128)} fusion(s32[2048]{0:T(1024)S(1)} %bitcast.67, bf16[2048,256]{1,0:T(8,128)(2,1)S(1)} %bitcast.59, f32[]{:T(128)} %constant.13.clone.1), kind=kCustom, calls=%fused_computation.7 | custom fusion | flops 1048576 | bytes 5242884 | tf_op jit(solution)/shard_map/scatter-add | solution.py:85
  166.0 9.9 %divide_subtract_fusion = (f32[4096,256]{1,0:T(8,128)}, f32[4096,256]{1,0:T(8,128)}) fusion(f32[4096,256]{1,0:T(8,128)} %param.14, f32[4096,256]{1,0:T(8,128)} %scatter_custom_fusion.2, f32[4096,256]{1,0:T(8,128)} %param.15), kind=kLoop, calls=%fused_computation.5 | loop fusion | flops 6291456 | bytes 20971520 | tf_op jit(solution)/shard_map/sub | solution.py:88
  (32 shorter events, 1.9 us)
Async XLA Ops:
  7.2 83.0 %copy-start = (bf16[256,256]{1,0:T(8,128)(2,1)S(1)}, bf16[256,256]{1,0:T(8,128)(2,1)}, u32[]{:S(2)}) copy-start(bf16[256,256]{1,0:T(8,128)(2,1)} %param.8) | copy-start | bytes 393220
  38.5 14.7 %copy-start.1 = (s32[256]{0:T(256)S(1)}, s32[256]{0:T(256)}, u32[]{:S(2)}) copy-start(s32[256]{0:T(256)} %param.11) | copy-start | bytes 3076
  49.2 28.8 %all-to-all-start.1 = ((bf16[32,64,256]{2,1,0:T(8,128)(2,1)}), bf16[32,64,256]{2,1,0:T(8,128)(2,1)S(1)}, u32[]{:S(2)}, u32[]{:S(2)}) async-start(bf16[32,64,256]{2,1,0:T(8,128)(2,1)} %bitcast.7), calls=%async_computation.1 | async-start | bytes 2097152 | tf_op jit(solution)/shard_map/all_to_all | solution.py:39
  51.9 60.7 %reduce-scatter.2.cloned.1.call-start = ((), (), s32[]{:S(2)}) async-start(), calls=%async_computation.4 | async-start | bytes 655360 | tf_op jit(solution)/shard_map/reduce_scatter | solution.py:64
  120.9 30.8 %all-to-all-start.2 = ((bf16[32,64,256]{2,1,0:T(8,128)(2,1)}), bf16[32,64,256]{2,1,0:T(8,128)(2,1)S(1)}, u32[]{:S(2)}, u32[]{:S(2)}) async-start(bf16[32,64,256]{2,1,0:T(8,128)(2,1)} %bitcast.11), calls=%async_computation.3 | async-start | bytes 2097152 | tf_op jit(solution)/shard_map/all_to_all | solution.py:79
Sparse Core Ops, SparseCore 0:
  92.1 20.4 reduce-scatter.1
where the time goes:
time: 184 us; the launch traced here: 183 us
  waiting for transfers between devices  70 us (38%)
  other arithmetic  42.6 us (23%)
  local copies, waits for them, and re-layouts  24 us (13%)
  blocking collectives  21.5 us (12%)
  between operations  15.5 us (8%)
  starting transfers between devices  7.29 us (4%)
    all_to_all x1, waiting for transfers between devices, per_device(): lax.all_to_all(outgoing.astype(jnp.bfloat16), ('shard', 'blk'), split_axi...  24.9 us
    all_to_all x1, waiting for transfers between devices, per_device(): lax.all_to_all(fetched_rows, ('shard', 'blk'), split_axis=0, concat_axis=...  24.7 us
    reduce_scatter x1, waiting for transfers between devices, per_device(): lax.psum_scatter(lax.dot_general(coef, query_vectors, (((0,), (0,)), ((),...  20.5 us
    all_to_all x1, blocking collectives, per_device(): lax.all_to_all(requests, ('shard', 'blk'), split_axis=0, concat_axis=0, t...  14.3 us
    scatter-add x1, other arithmetic, per_device(): row_gradient = jnp.zeros_like(item_embedding_matrix).at[wanted.reshape(-1...  14.3 us
    gather x1, local copies, waits for them, and re-layouts, per_device(): fetched_rows = item_embedding_matrix[wanted].astype(jnp.bfloat16)  10.7 us
    sub x1, other arithmetic, per_device(): item_embedding_matrix - LEARN_RATE * row_gradient / (jnp.sqrt(new_square_...  9.93 us
    another operation x2, other arithmetic  9.04 us
  transfers between devices with their start and end apart: 3, of which 3 were waited for; matrix products, arithmetic and copies ran while one was open for 1% of the time, Pallas kernels for 0%

commit v1 on v0

v1 whole, which is shorter than its diff:
```python
import functools

import jax
import jax.numpy as jnp
from jax import lax
from jax.experimental import pallas as pl
from jax.experimental.pallas import tpu as pltpu
from jax.sharding import PartitionSpec as P

LEARN_RATE = 0.5
ADAGRAD_EPSILON = 1e-08

BF16 = jnp.bfloat16
F32 = jnp.float32
I32 = jnp.int32
NT = (((1,), (1,)), ((), ()))
NN = (((1,), (0,)), ((), ()))


def dot(a, b, dims=NN):
    return lax.dot_general(a, b, dims, preferred_element_type=F32)


def one_hot(mask):
    return jnp.where(mask, 1.0, 0.0).astype(BF16)


def slot_matrix(ranks, capacity):
    devices, examples = ranks.shape
    place = lax.broadcasted_iota(I32, (capacity, examples), 0)
    return jnp.concatenate(
        [one_hot(ranks[o : o + 1, :] == place) for o in range(devices)], axis=0
    )


def ranks_of(owners, tally):
    bag, examples = owners.shape
    devices = tally[1]
    device = lax.broadcasted_iota(I32, (devices, examples), 0)
    named = jnp.zeros((devices, examples), I32)
    listed = jnp.zeros((devices, examples), I32)
    for k in range(bag):
        hit = jnp.where(owners[k : k + 1, :] == device, 1, 0)
        named = named + hit
        listed = listed + jnp.where(k < tally[0], hit, 0)
    earlier = one_hot(
        lax.broadcasted_iota(I32, (examples, examples), 0)
        < lax.broadcasted_iota(I32, (examples, examples), 1)
    )
    rank = dot(named.astype(F32).astype(BF16), earlier).astype(I32)
    return jnp.where(named > 0, rank, -1), jnp.where(listed > 0, rank, -1)


def route_kernel(owners_ref, rows_ref, tally_ref, requests_ref, listed_ref):
    devices, capacity = requests_ref.shape
    owners = owners_ref[...]
    rows = rows_ref[...]
    bag, examples = owners.shape
    named_rank, listed_rank = ranks_of(owners, (tally_ref[...], devices))
    listed_ref[...] = listed_rank
    slots = slot_matrix(named_rank, capacity)
    values = jnp.concatenate([rows >> 6, rows & 63, owners + 1], axis=0)
    values = jnp.concatenate([values, jnp.zeros((16 - 3 * bag, examples), I32)], axis=0)
    picked = dot(values.astype(F32).astype(BF16), slots, NT)
    owner = (lax.broadcasted_iota(I32, (1, devices * capacity), 1) // capacity + 1).astype(F32)
    found = jnp.zeros((1, devices * capacity), F32)
    for k in range(bag):
        row = picked[k : k + 1] * 64.0 + picked[bag + k : bag + k + 1] + 1.0
        found = found + jnp.where(picked[2 * bag + k : 2 * bag + k + 1] == owner, row, 0.0)
    found = found.astype(I32) - 1
    for o in range(devices):
        requests_ref[o : o + 1, :] = found[:, o * capacity : (o + 1) * capacity]


def prepare_kernel(listed_ref, tally_ref, into_ref, out_ref, share_ref, *, capacity):
    examples = listed_ref.shape[1]
    slots = slot_matrix(listed_ref[...], capacity)
    into_ref[...] = slots
    same = one_hot(
        lax.broadcasted_iota(I32, (examples, examples), 0)
        == lax.broadcasted_iota(I32, (examples, examples), 1)
    )
    out_ref[...] = dot(same, slots, NT).astype(BF16)
    share = 1.0 / tally_ref[...].astype(F32)
    share_ref[...] = jnp.broadcast_to(share, (128, examples)).T


def fetch_kernel(wanted_ref, table_ref, rows_ref, column_ref, *, step_rows):
    devices, capacity = wanted_ref.shape
    slots = devices * capacity
    width = table_ref.shape[0]
    block = pl.program_id(0)

    @pl.when(block == 0)
    def _():
        turned = wanted_ref[...].astype(F32).T.astype(I32)
        for s in range(devices):
            column_ref[s * capacity : (s + 1) * capacity, :] = jnp.broadcast_to(
                turned[:, s : s + 1], (capacity, 128)
            )
        rows_ref[...] = jnp.zeros(rows_ref.shape, BF16)

    table = table_ref[...].astype(BF16)
    lane = lax.broadcasted_iota(I32, (step_rows, 128), 1) + block * width
    for m in range(0, slots, step_rows):
        ids = column_ref[m : m + step_rows, :] - lane
        hot = jnp.concatenate([one_hot(ids == t) for t in range(0, width, 128)], axis=1)
        rows_ref[m : m + step_rows, :] += dot(hot, table).astype(BF16)


def loss_kernel(scale_ref, offset_ref, answered_ref, into_ref, out_ref, share_ref, *rest):
    queries, sent_ref = rest[:-1], rest[-1]
    examples, width = queries[0].shape
    scale = scale_ref[0]
    offset = offset_ref[0]
    grad_scale = scale / (examples * len(queries))
    share = jnp.concatenate([share_ref[...]] * (width // 128), axis=1)
    items = (dot(out_ref[...], answered_ref[...]) * share).astype(BF16)
    grad = jnp.zeros((examples, width), F32)
    for part, query_ref in enumerate(queries):
        query = query_ref[...]
        chance = jax.nn.sigmoid(scale * dot(items, query, NT) + offset)
        if part == 0:
            own = lax.broadcasted_iota(I32, (examples, examples), 0) == lax.broadcasted_iota(
                I32, (examples, examples), 1
            )
            chance = chance - jnp.where(own, 1.0, 0.0)
        grad = grad + dot((chance * grad_scale).astype(BF16), query)
    sent_ref[...] = dot(into_ref[...], (grad * share).astype(BF16)).astype(BF16)


def update_kernel(wanted_ref, incoming_ref, table_ref, energy_ref, table_out_ref, energy_out_ref, row_ref):
    devices, capacity = wanted_ref.shape
    block_rows = table_ref.shape[0]
    block = pl.program_id(0)

    @pl.when(block == 0)
    def _():
        for s in range(devices):
            row_ref[:, s * capacity : (s + 1) * capacity] = jnp.broadcast_to(
                wanted_ref[s : s + 1, :], (8, capacity)
            )

    place = lax.broadcasted_iota(I32, (block_rows, 128), 0) + block * block_rows
    hot = jnp.concatenate(
        [
            one_hot(jnp.broadcast_to(row_ref[0:1, c : c + 128], (block_rows, 128)) == place)
            for c in range(0, devices * capacity, 128)
        ],
        axis=1,
    )
    grad = dot(hot, incoming_ref[...])
    energy = energy_ref[...] + grad * grad
    energy_out_ref[...] = energy
    table_out_ref[...] = table_ref[...] - LEARN_RATE * grad / (jnp.sqrt(energy) + ADAGRAD_EPSILON)


def per_device(
    query_vectors,
    holding_devices,
    local_slot_number,
    valid_item_tally,
    score_stretch,
    offset_term,
    item_embedding_matrix,
    running_grad_energy,
):
    axes = ("shard", "blk")
    examples, bag = holding_devices.shape
    table_rows, width = item_embedding_matrix.shape
    devices = lax.axis_size(axes)
    blocks = lax.axis_size("blk")
    capacity = max(2, 2 * examples * bag // devices)
    slots = devices * capacity
    exchange = functools.partial(
        lax.all_to_all, axis_name=axes, split_axis=0, concat_axis=0, tiled=True
    )
    params = pltpu.CompilerParams(vmem_limit_bytes=40 * 1024 * 1024)
    tally = valid_item_tally.reshape(1, examples)

    requests, listed = pl.pallas_call(
        route_kernel,
        out_shape=(
            jax.ShapeDtypeStruct((devices, capacity), I32),
            jax.ShapeDtypeStruct((devices, examples), I32),
        ),
        name="route",
    )(holding_devices.T, local_slot_number.T, tally)
    wanted = exchange(requests)

    queries = [query_vectors]
    for step in range(1, blocks):
        queries.append(
            lax.ppermute(query_vectors, "blk", [(b, (b + step) % blocks) for b in range(blocks)])
        )
    into, out, share = pl.pallas_call(
        functools.partial(prepare_kernel, capacity=capacity),
        out_shape=(
            jax.ShapeDtypeStruct((slots, examples), BF16),
            jax.ShapeDtypeStruct((examples, slots), BF16),
            jax.ShapeDtypeStruct((examples, 128), F32),
        ),
        name="prepare",
    )(listed, tally)

    block = 1024
    fetched = pl.pallas_call(
        functools.partial(fetch_kernel, step_rows=256),
        grid=(table_rows // block,),
        in_specs=[
            pl.BlockSpec((devices, capacity), lambda i: (0, 0)),
            pl.BlockSpec((block, width), lambda i: (i, 0)),
        ],
        out_specs=pl.BlockSpec((slots, width), lambda i: (0, 0)),
        out_shape=jax.ShapeDtypeStruct((slots, width), BF16),
        scratch_shapes=[pltpu.VMEM((slots, 128), I32)],
        compiler_params=params,
        name="fetch",
    )(wanted, item_embedding_matrix)
    answered = exchange(fetched.reshape(devices, capacity, width)).reshape(slots, width)

    smem = pl.BlockSpec(memory_space=pltpu.SMEM)
    vmem = pl.BlockSpec(memory_space=pltpu.VMEM)
    sent = pl.pallas_call(
        loss_kernel,
        in_specs=[smem, smem] + [vmem] * (4 + blocks),
        out_shape=jax.ShapeDtypeStruct((slots, width), BF16),
        compiler_params=params,
        name="loss",
    )(score_stretch, offset_term, answered, into, out, share, *queries)
    incoming = exchange(sent.reshape(devices, capacity, width)).reshape(slots, width)

    block = 512
    rows = pl.BlockSpec((block, width), lambda i: (i, 0))
    return pl.pallas_call(
        update_kernel,
        grid=(table_rows // block,),
        in_specs=[
            pl.BlockSpec((devices, capacity), lambda i: (0, 0)),
            pl.BlockSpec((slots, width), lambda i: (0, 0)),
            rows,
            rows,
        ],
        out_specs=(rows, rows),
        out_shape=(
            jax.ShapeDtypeStruct((table_rows, width), F32),
            jax.ShapeDtypeStruct((table_rows, width), F32),
        ),
        scratch_shapes=[pltpu.VMEM((8, slots), I32)],
        compiler_params=params,
        name="update",
    )(wanted, incoming, item_embedding_matrix, running_grad_energy)


def solution(mesh):
    rows = P(("shard", "blk"), None)
    placed = (rows, rows, rows, P(("shard", "blk")), P(), P(), rows, rows)
    return jax.shard_map(
        per_device, mesh=mesh, in_specs=placed, out_specs=(rows, rows), check_vma=False
    )
```

time: 184 us -> 100 us (0.54)
  waiting for transfers between devices: 70 us -> 18.9 us
  other arithmetic: 42.6 us -> 0 us
  blocking collectives: 21.5 us -> 44 us
  Pallas kernels: 0 us -> 21 us
  local copies, waits for them, and re-layouts: 24 us -> 8.09 us
  between operations: 15.5 us -> 1.96 us
    all_to_all x2 -> x1, waiting for transfers between devices: 49.6 us -> 9.35 us  [per_device(): exchange(fetched.reshape(devices, capacity, width)).reshape(slots, width)]
    all_to_all x1 -> x2, blocking collectives: 14.3 us -> 44 us  [the longest x1 29.6 us: per_device(): exchange(sent.reshape(devices, capacity, width)).reshape(slots, width)]
    pallas_call x0 -> x5, Pallas kernels: none -> 21 us  [the longest x1 8.08 us: per_device(): pl.pallas_call(update_kernel, grid=(table_rows // block,), in_specs=[pl.B...]
    reduce_scatter x1 -> x0, waiting for transfers between devices: 20.5 us -> none  [per_device(): lax.psum_scatter(lax.dot_general(coef, query_vectors, (((0,), (0,)), ((),...]
    gather x2 -> x0, local copies, waits for them, and re-layouts: 14.6 us -> none  [the longest x1 10.7 us: per_device(): fetched_rows = item_embedding_matrix[wanted].astype(jnp.bfloat16)]
    scatter-add x1 -> x0, other arithmetic: 14.3 us -> none  [per_device(): row_gradient = jnp.zeros_like(item_embedding_matrix).at[wanted.reshape(-1...]
    sub x2 -> x0, other arithmetic: 10 us -> none  [the longest x1 9.93 us: per_device(): item_embedding_matrix - LEARN_RATE * row_gradient / (jnp.sqrt(new_square_...]
    ppermute x0 -> x3, waiting for transfers between devices: none -> 9.52 us  [per_device(): lax.ppermute(query_vectors, 'blk', [(b, (b + step) % blocks) for b in ran...]
  transfers between devices with their start and end apart: 3 -> 4, of which waited for: 3 -> 3; matrix products, arithmetic and copies ran while one was open for 1% -> 0% of each run, Pallas kernels for 0% -> 3%
where the time goes in v1:
time: 100 us
  blocking collectives  44 us (44%)
  Pallas kernels  21 us (21%)
  waiting for transfers between devices  18.9 us (19%)
  local copies, waits for them, and re-layouts  8.09 us (8%)
  starting transfers between devices  6.11 us (6%)
  between operations  1.96 us (2%)
    all_to_all x1, blocking collectives, per_device(): exchange(sent.reshape(devices, capacity, width)).reshape(slots, width)  29.6 us
    all_to_all x1, blocking collectives, per_device(): wanted = exchange(requests)  14.4 us
    ppermute x3, waiting for transfers between devices, per_device(): lax.ppermute(query_vectors, 'blk', [(b, (b + step) % blocks) for b in ran...  9.52 us
    all_to_all x1, waiting for transfers between devices, per_device(): exchange(fetched.reshape(devices, capacity, width)).reshape(slots, width)  9.35 us
    unnamed x14, local copies, waits for them, and re-layouts  8.09 us
    pallas_call x1, Pallas kernels, per_device(): pl.pallas_call(update_kernel, grid=(table_rows // block,), in_specs=[pl.B...  8.08 us
    pallas_call x1, Pallas kernels, per_device(): pl.pallas_call(functools.partial(fetch_kernel, step_rows=256), grid=(tabl...  6.53 us
    ppermute x3, starting transfers between devices, per_device(): lax.ppermute(query_vectors, 'blk', [(b, (b + step) % blocks) for b in ran...  3.46 us
  transfers between devices with their start and end apart: 4, of which 3 were waited for; matrix products, arithmetic and copies ran while one was open for 0% of the time, Pallas kernels for 3%

profile of v1, /device:TPU:0, one launch (start us, length us, event | category | flops | bytes accessed | tf_op | source)
XLA Modules:
  0.0 100.0 jit_solution(9560642817406368060)
XLA Ops:
  0.6 1.9 %route.1 = (s32[32,64]{1,0:T(8,128)}, s32[32,256]{1,0:T(8,128)}) custom-call(s32[4,256]{1,0:T(4,128)} %bitcast.19, s32[4,256]{1,0:T(4,128)} %bitcast.20, s32[1,256]{1,0:T(1,128)} %bitcast.17), custom_call_target="tpu_custom_call" | custom-call | tf_op jit(solution)/shard_map/route/pallas_call | solution.py:181
  2.6 14.4 %all_to_all.21 = s32[32,1,64]{2,1,0:T(1,128)S(1)} all-to-all(s32[32,1,64]{2,1,0:T(1,128)} %bitcast.16), channel_id=1, replica_groups=mesh['shard'=8,'blk'=4] {'shard','blk'}, dimensions={0} | all-to-all | bytes 16384 | tf_op jit(solution)/shard_map/all_to_all | solution.py:189
  17.0 0.0 copy-start
  17.0 2.2 %copy-done = f32[4096,256]{1,0:T(8,128)S(1)} copy-done((f32[4096,256]{1,0:T(8,128)S(1)}, f32[4096,256]{1,0:T(8,128)}, u32[]{:S(2)}) %copy-start) | copy-done | bytes 4194328
  19.2 0.0 copy-start.5
  19.2 6.5 %fetch.1 = bf16[2048,256]{1,0:T(8,128)(2,1)} custom-call(s32[32,64]{1,0:T(8,128)S(1)} %bitcast.14, f32[4096,256]{1,0:T(8,128)S(1)} %copy-done), custom_call_target="tpu_custom_call" | custom-call | tf_op jit(solution)/shard_map/fetch/pallas_call | solution.py:207
  25.7 2.6 %all-to-all-start.1 = ((bf16[32,64,256]{2,1,0:T(8,128)(2,1)}), bf16[32,64,256]{2,1,0:T(8,128)(2,1)S(1)}, u32[]{:S(2)}, u32[]{:S(2)}) async-start(bf16[32,64,256]{2,1,0:T(8,128)(2,1)} %bitcast.6), calls=%async_computation.1 | async-start | bytes 2097152 | tf_op jit(solution)/shard_map/all_to_all | solution.py:220
  28.4 0.0 copy-done.5
  28.4 1.7 %collective-permute-start.1 = (bf16[256,256]{1,0:T(8,128)(2,1)S(1)}, bf16[256,256]{1,0:T(8,128)(2,1)S(1)}, u32[]{:S(2)}, u32[]{:S(2)}) collective-permute-start(bf16[256,256]{1,0:T(8,128)(2,1)S(1)} %copy-done.5), channel_id=1, source_target_pairs={{0,2},{1,3},{2,0},{3,1},{4,6},{5,7},{6,4},{7,5},{8,10},{9,11},{10,... | collective-permute-start | bytes 393224 | tf_op jit(solution)/shard_map/ppermute | solution.py:194
  30.1 0.0 collective-permute-start
  30.1 1.7 %collective-permute-start.2 = (bf16[256,256]{1,0:T(8,128)(2,1)S(1)}, bf16[256,256]{1,0:T(8,128)(2,1)S(1)}, u32[]{:S(2)}, u32[]{:S(2)}) collective-permute-start(bf16[256,256]{1,0:T(8,128)(2,1)S(1)} %copy-done.5), channel_id=1, source_target_pairs={{0,3},{1,0},{2,1},{3,2},{4,7},{5,4},{6,5},{7,6},{8,11},{9,8},{10,9... | collective-permute-start | bytes 393224 | tf_op jit(solution)/shard_map/ppermute | solution.py:194
  33.2 2.5 %prepare.1 = (bf16[2048,256]{1,0:T(8,128)(2,1)}, bf16[256,2048]{1,0:T(8,128)(2,1)}, f32[256,128]{1,0:T(8,128)}) custom-call(s32[32,256]{1,0:T(8,128)} %get-tuple-element.8.listed_ref, s32[1,256]{1,0:T(1,128)} %bitcast.18), custom_call_target="tpu_custom_call" | custom-call | tf_op jit(solution)/shard_map/prepare/pallas_call | solution.py:196
  35.7 6.9 %collective-permute-done.1.rest_2_ = bf16[256,256]{1,0:T(8,128)(2,1)S(1)} collective-permute-done((bf16[256,256]{1,0:T(8,128)(2,1)S(1)}, bf16[256,256]{1,0:T(8,128)(2,1)S(1)}, u32[]{:S(2)}, u32[]{:S(2)}) %collective-permute-start.1) | collective-permute-done | bytes 131104 | tf_op jit(solution)/shard_map/ppermute | solution.py:194
  42.6 2.7 %collective-permute-done.rest_1_ = bf16[256,256]{1,0:T(8,128)(2,1)S(1)} collective-permute-done((bf16[256,256]{1,0:T(8,128)(2,1)S(1)}, bf16[256,256]{1,0:T(8,128)(2,1)S(1)}, u32[]{:S(2)}, u32[]{:S(2)}) %collective-permute-start) | collective-permute-done | bytes 131104 | tf_op jit(solution)/shard_map/ppermute | solution.py:194
  45.2 0.0 collective-permute-done.2.rest_3_
  45.2 9.4 %all-to-all-done.1 = bf16[32,64,256]{2,1,0:T(8,128)(2,1)S(1)} async-done(((bf16[32,64,256]{2,1,0:T(8,128)(2,1)}), bf16[32,64,256]{2,1,0:T(8,128)(2,1)S(1)}, u32[]{:S(2)}, u32[]{:S(2)}) %all-to-all-start.1) | async-done | bytes 1048608 | tf_op jit(solution)/shard_map/all_to_all | solution.py:220
  54.6 1.4 %copy-done.3 = bf16[2048,256]{1,0:T(8,128)(2,1)S(1)} copy-done((bf16[2048,256]{1,0:T(8,128)(2,1)S(1)}, bf16[2048,256]{1,0:T(8,128)(2,1)}, u32[]{:S(2)}) %copy-start.3) | copy-done | bytes 1048600
  55.9 1.4 %copy-done.4 = bf16[256,2048]{1,0:T(8,128)(2,1)S(1)} copy-done((bf16[256,2048]{1,0:T(8,128)(2,1)S(1)}, bf16[256,2048]{1,0:T(8,128)(2,1)}, u32[]{:S(2)}) %copy-start.4) | copy-done | bytes 1048600
  57.4 0.9 copy-done.6
  58.3 1.9 %loss.1 = bf16[2048,256]{1,0:T(8,128)(2,1)S(1)} custom-call(f32[1]{0:T(128)S(6)} %copy.11.scale_ref, f32[1]{0:T(128)S(6)} %copy.12.offset_ref, bf16[2048,256]{1,0:T(8,128)(2,1)S(1)} %bitcast.12, bf16[2048,256]{1,0:T(8,128)(2,1)S(1)} %copy-done.3, bf16[256,2048]{1,0:T(8,128)(2,1)S(1)} %copy-done.4, f32[256,128]{1,0:T(8,128)S(1)} %copy-done.6, ...), custom_call_target="tpu_custom_call" | custom-call | tf_op jit(solution)/shard_map/loss/pallas_call | solution.py:224
  60.2 29.6 %all_to_all.22 = bf16[32,64,256]{2,1,0:T(8,128)(2,1)S(1)} all-to-all(bf16[32,64,256]{2,1,0:T(8,128)(2,1)S(1)} %bitcast.13), channel_id=1, replica_groups=mesh['shard'=8,'blk'=4] {'shard','blk'}, dimensions={0} | all-to-all | bytes 2097152 | tf_op jit(solution)/shard_map/all_to_all | solution.py:231
  89.7 0.0 copy-done.1
  89.7 2.2 %copy-done.2 = f32[4096,256]{1,0:T(8,128)S(1)} copy-done((f32[4096,256]{1,0:T(8,128)S(1)}, f32[4096,256]{1,0:T(8,128)}, u32[]{:S(2)}) %copy-start.2) | copy-done | bytes 4194328
  91.9 8.1 %update.1 = (f32[4096,256]{1,0:T(8,128)}, f32[4096,256]{1,0:T(8,128)}) custom-call(s32[32,64]{1,0:T(8,128)S(1)} %bitcast.15, bf16[2048,256]{1,0:T(8,128)(2,1)S(1)} %bitcast.11, f32[4096,256]{1,0:T(8,128)S(1)} %copy-done.1, f32[4096,256]{1,0:T(8,128)S(1)} %copy-done.2), custom_call_target="tpu_custom_call" | custom-call | tf_op jit(solution)/shard_map/update/pallas_call | solution.py:235
  (5 shorter events, 0.0 us)
Async XLA Ops:
  17.0 2.2 %copy-start = (f32[4096,256]{1,0:T(8,128)S(1)}, f32[4096,256]{1,0:T(8,128)}, u32[]{:S(2)}) copy-start(f32[4096,256]{1,0:T(8,128)} %table_ref.3) | copy-start | bytes 12582916
  19.2 9.2 %copy-start.5 = (bf16[256,256]{1,0:T(8,128)(2,1)S(1)}, bf16[256,256]{1,0:T(8,128)(2,1)}, u32[]{:S(2)}) copy-start(bf16[256,256]{1,0:T(8,128)(2,1)} %rest_0_.1) | copy-start | bytes 393220
  25.7 28.8 %all-to-all-start.1 = ((bf16[32,64,256]{2,1,0:T(8,128)(2,1)}), bf16[32,64,256]{2,1,0:T(8,128)(2,1)S(1)}, u32[]{:S(2)}, u32[]{:S(2)}) async-start(bf16[32,64,256]{2,1,0:T(8,128)(2,1)} %bitcast.6), calls=%async_computation.1 | async-start | bytes 2097152 | tf_op jit(solution)/shard_map/all_to_all | solution.py:220
  28.4 14.2 %collective-permute-start.1 = (bf16[256,256]{1,0:T(8,128)(2,1)S(1)}, bf16[256,256]{1,0:T(8,128)(2,1)S(1)}, u32[]{:S(2)}, u32[]{:S(2)}) collective-permute-start(bf16[256,256]{1,0:T(8,128)(2,1)S(1)} %copy-done.5), channel_id=1, source_target_pairs={{0,2},{1,3},{2,0},{3,1},{4,6},{5,7},{6,4},{7,5},{8,10},{9,11},{10,... | collective-permute-start | bytes 393224 | tf_op jit(solution)/shard_map/ppermute | solution.py:194
  30.1 15.1 %collective-permute-start = (bf16[256,256]{1,0:T(8,128)(2,1)S(1)}, bf16[256,256]{1,0:T(8,128)(2,1)S(1)}, u32[]{:S(2)}, u32[]{:S(2)}) collective-permute-start(bf16[256,256]{1,0:T(8,128)(2,1)S(1)} %copy-done.5), channel_id=1, source_target_pairs={{0,1},{1,2},{2,3},{3,0},{4,5},{5,6},{6,7},{7,4},{8,9},{9,10},{10,1... | collective-permute-start | bytes 393224 | tf_op jit(solution)/shard_map/ppermute | solution.py:194
  30.1 15.1 %collective-permute-start.2 = (bf16[256,256]{1,0:T(8,128)(2,1)S(1)}, bf16[256,256]{1,0:T(8,128)(2,1)S(1)}, u32[]{:S(2)}, u32[]{:S(2)}) collective-permute-start(bf16[256,256]{1,0:T(8,128)(2,1)S(1)} %copy-done.5), channel_id=1, source_target_pairs={{0,3},{1,0},{2,1},{3,2},{4,7},{5,4},{6,5},{7,6},{8,11},{9,8},{10,9... | collective-permute-start | bytes 393224 | tf_op jit(solution)/shard_map/ppermute | solution.py:194
  54.6 35.2 %copy-start.1 = (f32[4096,256]{1,0:T(8,128)S(1)}, f32[4096,256]{1,0:T(8,128)}, u32[]{:S(2)}) copy-start(f32[4096,256]{1,0:T(8,128)} %table_ref.3) | copy-start | bytes 12582916
  54.6 1.4 %copy-start.3 = (bf16[2048,256]{1,0:T(8,128)(2,1)S(1)}, bf16[2048,256]{1,0:T(8,128)(2,1)}, u32[]{:S(2)}) copy-start(bf16[2048,256]{1,0:T(8,128)(2,1)} %get-tuple-element.9.into_ref) | copy-start | bytes 3145732
  55.9 1.4 %copy-start.4 = (bf16[256,2048]{1,0:T(8,128)(2,1)S(1)}, bf16[256,2048]{1,0:T(8,128)(2,1)}, u32[]{:S(2)}) copy-start(bf16[256,2048]{1,0:T(8,128)(2,1)} %get-tuple-element.10.out_ref) | copy-start | bytes 3145732
  57.4 0.9 copy-start.6
  89.7 2.2 %copy-start.2 = (f32[4096,256]{1,0:T(8,128)S(1)}, f32[4096,256]{1,0:T(8,128)}, u32[]{:S(2)}) copy-start(f32[4096,256]{1,0:T(8,128)} %energy_ref.1) | copy-start | bytes 12582916

commit v2 on v1

--- a/solution.py
+++ b/solution.py
@@ -85,40 +85,44 @@
     share_ref[...] = jnp.broadcast_to(share, (128, examples)).T
 
 
-def fetch_kernel(wanted_ref, table_ref, rows_ref, column_ref, *, step_rows):
+def fetch_kernel(wanted_ref, table_ref, rows_ref, column_ref, *, step_rows, block):
     devices, capacity = wanted_ref.shape
     slots = devices * capacity
-    width = table_ref.shape[0]
-    block = pl.program_id(0)
-
-    @pl.when(block == 0)
-    def _():
-        turned = wanted_ref[...].astype(F32).T.astype(I32)
-        for s in range(devices):
-            column_ref[s * capacity : (s + 1) * capacity, :] = jnp.broadcast_to(
-                turned[:, s : s + 1], (capacity, 128)
+    turned = wanted_ref[...].astype(F32).T.astype(I32)
+    for s in range(devices):
+        column_ref[s * capacity : (s + 1) * capacity, :] = jnp.broadcast_to(
+            turned[:, s : s + 1], (capacity, 128)
+        )
+    lane = lax.broadcasted_iota(I32, (step_rows, 128), 1)
+    for b in range(table_ref.shape[0] // block):
+        table = table_ref[b * block : (b + 1) * block, :].astype(BF16)
+        for m in range(0, slots, step_rows):
+            ids = column_ref[m : m + step_rows, :] - lane
+            hot = jnp.concatenate(
+                [one_hot(ids == b * block + t) for t in range(0, block, 128)], axis=1
             )
-        rows_ref[...] = jnp.zeros(rows_ref.shape, BF16)
-
-    table = table_ref[...].astype(BF16)
-    lane = lax.broadcasted_iota(I32, (step_rows, 128), 1) + block * width
-    for m in range(0, slots, step_rows):
-        ids = column_ref[m : m + step_rows, :] - lane
-        hot = jnp.concatenate([one_hot(ids == t) for t in range(0, width, 128)], axis=1)
-        rows_ref[m : m + step_rows, :] += dot(hot, table).astype(BF16)
+            rows = dot(hot, table).astype(BF16)
+            rows_ref[m : m + step_rows, :] = rows if b == 0 else rows_ref[m : m + step_rows, :] + rows
 
 
 def loss_kernel(scale_ref, offset_ref, answered_ref, into_ref, out_ref, share_ref, *rest):
-    queries, sent_ref = rest[:-1], rest[-1]
+    queries, (sent_ref, query_ref, arrived) = rest[:-3], rest[-3:]
     examples, width = queries[0].shape
+    loads = [
+        pltpu.make_async_copy(query, query_ref.at[part], arrived.at[part])
+        for part, query in enumerate(queries)
+    ]
+    for load in loads:
+        load.start()
     scale = scale_ref[0]
     offset = offset_ref[0]
     grad_scale = scale / (examples * len(queries))
     share = jnp.concatenate([share_ref[...]] * (width // 128), axis=1)
     items = (dot(out_ref[...], answered_ref[...]) * share).astype(BF16)
     grad = jnp.zeros((examples, width), F32)
-    for part, query_ref in enumerate(queries):
-        query = query_ref[...]
+    for part, load in enumerate(loads):
+        load.wait()
+        query = query_ref[part]
         chance = jax.nn.sigmoid(scale * dot(items, query, NT) + offset)
         if part == 0:
             own = lax.broadcasted_iota(I32, (examples, examples), 0) == lax.broadcasted_iota(
@@ -129,30 +133,53 @@
     sent_ref[...] = dot(into_ref[...], (grad * share).astype(BF16)).astype(BF16)
 
 
-def update_kernel(wanted_ref, incoming_ref, table_ref, energy_ref, table_out_ref, energy_out_ref, row_ref):
+def update_kernel(
+    wanted_ref, incoming_ref, table_ref, energy_ref, table_out_ref, energy_out_ref,
+    row_ref, table_buf, energy_buf, table_sem, energy_sem,
+):
     devices, capacity = wanted_ref.shape
-    block_rows = table_ref.shape[0]
-    block = pl.program_id(0)
-
-    @pl.when(block == 0)
-    def _():
-        for s in range(devices):
-            row_ref[:, s * capacity : (s + 1) * capacity] = jnp.broadcast_to(
-                wanted_ref[s : s + 1, :], (8, capacity)
-            )
-
-    place = lax.broadcasted_iota(I32, (block_rows, 128), 0) + block * block_rows
-    hot = jnp.concatenate(
-        [
-            one_hot(jnp.broadcast_to(row_ref[0:1, c : c + 128], (block_rows, 128)) == place)
-            for c in range(0, devices * capacity, 128)
-        ],
-        axis=1,
-    )
-    grad = dot(hot, incoming_ref[...])
-    energy = energy_ref[...] + grad * grad
-    energy_out_ref[...] = energy
-    table_out_ref[...] = table_ref[...] - LEARN_RATE * grad / (jnp.sqrt(energy) + ADAGRAD_EPSILON)
+    slots, _ = incoming_ref.shape
+    block = table_buf.shape[1]
+    blocks = table_ref.shape[0] // block
+    for s in range(devices):
+        row_ref[:, s * capacity : (s + 1) * capacity] = jnp.broadcast_to(
+            wanted_ref[s : s + 1, :], (8, capacity)
+        )
+    place = lax.broadcasted_iota(I32, (block, 128), 0)
+
+    def stores(b, half):
+        at = pl.ds(pl.multiple_of(b * block, block), block)
+        return (
+            pltpu.make_async_copy(table_buf.at[half], table_out_ref.at[at, :], table_sem.at[half]),
+            pltpu.make_async_copy(energy_buf.at[half], energy_out_ref.at[at, :], energy_sem.at[half]),
+        )
+
+    def step(b, half):
+        at = pl.ds(pl.multiple_of(b * block, block), block)
+        here = place + b * block
+        hot = jnp.concatenate(
+            [
+                one_hot(jnp.broadcast_to(row_ref[0:1, c : c + 128], (block, 128)) == here)
+                for c in range(0, slots, 128)
+            ],
+            axis=1,
+        )
+        grad = dot(hot, incoming_ref[...])
+        energy = energy_ref[at, :] + grad * grad
+        energy_buf[half] = energy
+        table_buf[half] = table_ref[at, :] - LEARN_RATE * grad / (jnp.sqrt(energy) + ADAGRAD_EPSILON)
+        for store in stores(b, half):
+            store.start()
+
+    for b in range(blocks):
+        half = b % 2
+        if b >= 2:
+            for store in stores(b - 2, half):
+                store.wait()
+        step(b, half)
+    for b in (blocks - 2, blocks - 1):
+        for store in stores(b, b % 2):
+            store.wait()
 
 
 def per_device(
@@ -175,7 +202,19 @@
     exchange = functools.partial(
         lax.all_to_all, axis_name=axes, split_axis=0, concat_axis=0, tiled=True
     )
-    params = pltpu.CompilerParams(vmem_limit_bytes=40 * 1024 * 1024)
+    smem = pl.BlockSpec(memory_space=pltpu.SMEM)
+    vmem = pl.BlockSpec(memory_space=pltpu.VMEM)
+    hbm = pl.BlockSpec(memory_space=pltpu.HBM)
+
+    def in_hbm(array):
+        return pltpu.with_memory_space_constraint(array, pltpu.HBM)
+
+    def limit(mib):
+        return pltpu.CompilerParams(vmem_limit_bytes=mib * 1024 * 1024)
+
+    def cost(gflops):
+        return pl.CostEstimate(flops=gflops * 10**9, transcendentals=0, bytes_accessed=10**6)
+
     tally = valid_item_tally.reshape(1, examples)
 
     requests, listed = pl.pallas_call(
@@ -184,8 +223,10 @@
             jax.ShapeDtypeStruct((devices, capacity), I32),
             jax.ShapeDtypeStruct((devices, examples), I32),
         ),
+        compiler_params=limit(4),
+        cost_estimate=cost(10),
         name="route",
-    )(holding_devices.T, local_slot_number.T, tally)
+    )(in_hbm(holding_devices.T), in_hbm(local_slot_number.T), in_hbm(tally))
     wanted = exchange(requests)
 
     queries = [query_vectors]
@@ -200,54 +241,51 @@
             jax.ShapeDtypeStruct((examples, slots), BF16),
             jax.ShapeDtypeStruct((examples, 128), F32),
         ),
+        compiler_params=limit(8),
         name="prepare",
-    )(listed, tally)
-
-    block = 1024
+    )(listed, in_hbm(tally))
+
     fetched = pl.pallas_call(
-        functools.partial(fetch_kernel, step_rows=256),
-        grid=(table_rows // block,),
-        in_specs=[
-            pl.BlockSpec((devices, capacity), lambda i: (0, 0)),
-            pl.BlockSpec((block, width), lambda i: (i, 0)),
-        ],
-        out_specs=pl.BlockSpec((slots, width), lambda i: (0, 0)),
+        functools.partial(fetch_kernel, step_rows=256, block=1024),
+        in_specs=[vmem, vmem],
         out_shape=jax.ShapeDtypeStruct((slots, width), BF16),
         scratch_shapes=[pltpu.VMEM((slots, 128), I32)],
-        compiler_params=params,
+        compiler_params=limit(12),
         name="fetch",
     )(wanted, item_embedding_matrix)
     answered = exchange(fetched.reshape(devices, capacity, width)).reshape(slots, width)
 
-    smem = pl.BlockSpec(memory_space=pltpu.SMEM)
-    vmem = pl.BlockSpec(memory_space=pltpu.VMEM)
     sent = pl.pallas_call(
         loss_kernel,
-        in_specs=[smem, smem] + [vmem] * (4 + blocks),
+        in_specs=[smem, smem] + [vmem] * 4 + [hbm] * blocks,
         out_shape=jax.ShapeDtypeStruct((slots, width), BF16),
-        compiler_params=params,
+        scratch_shapes=[
+            pltpu.VMEM((blocks, examples, width), BF16),
+            pltpu.SemaphoreType.DMA((blocks,)),
+        ],
+        compiler_params=limit(12),
+        cost_estimate=cost(30),
         name="loss",
-    )(score_stretch, offset_term, answered, into, out, share, *queries)
+    )(score_stretch, offset_term, answered, into, out, share, *map(in_hbm, queries))
     incoming = exchange(sent.reshape(devices, capacity, width)).reshape(slots, width)
 
     block = 512
-    rows = pl.BlockSpec((block, width), lambda i: (i, 0))
     return pl.pallas_call(
         update_kernel,
-        grid=(table_rows // block,),
-        in_specs=[
-            pl.BlockSpec((devices, capacity), lambda i: (0, 0)),
-            pl.BlockSpec((slots, width), lambda i: (0, 0)),
-            rows,
-            rows,
-        ],
-        out_specs=(rows, rows),
+        in_specs=[vmem] * 4,
+        out_specs=(hbm, hbm),
         out_shape=(
             jax.ShapeDtypeStruct((table_rows, width), F32),
             jax.ShapeDtypeStruct((table_rows, width), F32),
         ),
-        scratch_shapes=[pltpu.VMEM((8, slots), I32)],
-        compiler_params=params,
+        scratch_shapes=[
+            pltpu.VMEM((8, slots), I32),
+            pltpu.VMEM((2, block, width), F32),
+            pltpu.VMEM((2, block, width), F32),
+            pltpu.SemaphoreType.DMA((2,)),
+            pltpu.SemaphoreType.DMA((2,)),
+        ],
+        compiler_params=limit(16),
         name="update",
     )(wanted, incoming, item_embedding_matrix, running_grad_energy)
 

time: 100 us -> 95.9 us (0.959)
  local copies, waits for them, and re-layouts: 8.09 us -> 0.68 us
  Pallas kernels: 21 us -> 23.5 us
    unnamed x14 -> x12, local copies, waits for them, and re-layouts: 8.09 us -> 0.68 us
    pallas_call x3, Pallas kernels: 16.5 us -> 20.6 us  [the longest x1 11.8 us: per_device(): pl.pallas_call(update_kernel, in_specs=[vmem] * 4, out_specs=(hbm, hbm),...]
    pallas_call x1, Pallas kernels: 2.54 us -> 1.38 us  [per_device(): pl.pallas_call(functools.partial(prepare_kernel, capacity=capacity), out_...]
    ppermute x3, waiting for transfers between devices: 9.52 us -> 10.7 us  [per_device(): lax.ppermute(query_vectors, 'blk', [(b, (b + step) % blocks) for b in ran...]
  transfers between devices with their start and end apart: 4 -> 4, of which waited for: 3 -> 3; matrix products, arithmetic and copies ran while one was open for 0% -> 0% of each run, Pallas kernels for 3% -> 1%
where the time goes in v2:
time: 95.9 us; the launch traced here: 95.6 us
  blocking collectives  43.9 us (46%)
  Pallas kernels  23.5 us (25%)
  waiting for transfers between devices  19.4 us (20%)
  starting transfers between devices  6.11 us (6%)
  between operations  2.14 us (2%)
    all_to_all x1, blocking collectives, per_device(): exchange(sent.reshape(devices, capacity, width)).reshape(slots, width)  29.6 us
    all_to_all x1, blocking collectives, per_device(): wanted = exchange(requests)  14.3 us
    pallas_call x1, Pallas kernels, per_device(): pl.pallas_call(update_kernel, in_specs=[vmem] * 4, out_specs=(hbm, hbm),...  11.8 us
    ppermute x3, waiting for transfers between devices, per_device(): lax.ppermute(query_vectors, 'blk', [(b, (b + step) % blocks) for b in ran...  10.7 us
    all_to_all x1, waiting for transfers between devices, per_device(): exchange(fetched.reshape(devices, capacity, width)).reshape(slots, width)  8.69 us
    pallas_call x1, Pallas kernels, per_device(): pl.pallas_call(functools.partial(fetch_kernel, step_rows=256, block=1024)...  5.64 us
    ppermute x3, starting transfers between devices, per_device(): lax.ppermute(query_vectors, 'blk', [(b, (b + step) % blocks) for b in ran...  3.46 us
    pallas_call x1, Pallas kernels, per_device(): pl.pallas_call(loss_kernel, in_specs=[smem, smem] + [vmem] * 4 + [hbm] *...  3.19 us
  transfers between devices with their start and end apart: 4, of which 3 were waited for; matrix products, arithmetic and copies ran while one was open for 0% of the time, Pallas kernels for 1%

profile of v2, /device:TPU:0, one launch (start us, length us, event | category | flops | bytes accessed | tf_op | source)
XLA Modules:
  0.0 95.6 jit_solution(16175327116516403067)
XLA Ops:
  0.6 0.0 copy-start
  0.6 1.5 %route.1 = (s32[32,64]{1,0:T(8,128)S(1)}, s32[32,256]{1,0:T(8,128)S(1)}) custom-call(s32[4,256]{1,0:T(4,128)} %bitcast.19, s32[4,256]{1,0:T(4,128)} %bitcast.20, s32[1,256]{1,0:T(1,128)} %bitcast.17), custom_call_target="tpu_custom_call" | custom-call | flops 10000000000 | bytes 1000000 | tf_op jit(solution)/shard_map/route/pallas_call | solution.py:220
  2.1 0.0 copy-start.3
  2.1 14.3 %all_to_all.21 = s32[32,1,64]{2,1,0:T(1,128)S(1)} all-to-all(s32[32,1,64]{2,1,0:T(1,128)S(1)} %bitcast.16), channel_id=1, replica_groups=mesh['shard'=8,'blk'=4] {'shard','blk'}, dimensions={0} | all-to-all | bytes 16384 | tf_op jit(solution)/shard_map/all_to_all | solution.py:230
  16.4 0.0 copy-done
  16.4 5.6 %fetch.1 = bf16[2048,256]{1,0:T(8,128)(2,1)} custom-call(s32[32,64]{1,0:T(8,128)S(1)} %bitcast.14, f32[4096,256]{1,0:T(8,128)S(1)} %copy-done), custom_call_target="tpu_custom_call" | custom-call | tf_op jit(solution)/shard_map/fetch/pallas_call | solution.py:248
  22.1 2.6 %all-to-all-start.1 = ((bf16[32,64,256]{2,1,0:T(8,128)(2,1)}), bf16[32,64,256]{2,1,0:T(8,128)(2,1)S(1)}, u32[]{:S(2)}, u32[]{:S(2)}) async-start(bf16[32,64,256]{2,1,0:T(8,128)(2,1)} %bitcast.6), calls=%async_computation.1 | async-start | bytes 2097152 | tf_op jit(solution)/shard_map/all_to_all | solution.py:256
  24.7 0.0 copy-done.3
  24.7 1.7 %collective-permute-start.1 = (bf16[256,256]{1,0:T(8,128)(2,1)S(1)}, bf16[256,256]{1,0:T(8,128)(2,1)S(1)}, u32[]{:S(2)}, u32[]{:S(2)}) collective-permute-start(bf16[256,256]{1,0:T(8,128)(2,1)S(1)} %copy-done.3), channel_id=1, source_target_pairs={{0,2},{1,3},{2,0},{3,1},{4,6},{5,7},{6,4},{7,5},{8,10},{9,11},{10,... | collective-permute-start | bytes 393224 | tf_op jit(solution)/shard_map/ppermute | solution.py:235
  26.5 0.0 collective-permute-start
  26.5 1.7 %collective-permute-start.2 = (bf16[256,256]{1,0:T(8,128)(2,1)S(1)}, bf16[256,256]{1,0:T(8,128)(2,1)}, u32[]{:S(2)}, u32[]{:S(2)}) collective-permute-start(bf16[256,256]{1,0:T(8,128)(2,1)S(1)} %copy-done.3), channel_id=1, source_target_pairs={{0,3},{1,0},{2,1},{3,2},{4,7},{5,4},{6,5},{7,6},{8,11},{9,8},{10,9... | collective-permute-start | bytes 393224 | tf_op jit(solution)/shard_map/ppermute | solution.py:235
  29.5 1.4 %prepare.1 = (bf16[2048,256]{1,0:T(8,128)(2,1)S(1)}, bf16[256,2048]{1,0:T(8,128)(2,1)S(1)}, f32[256,128]{1,0:T(8,128)S(1)}) custom-call(s32[32,256]{1,0:T(8,128)S(1)} %get-tuple-element.8.listed_ref, s32[1,256]{1,0:T(1,128)} %bitcast.18), custom_call_target="tpu_custom_call" | custom-call | tf_op jit(solution)/shard_map/prepare/pallas_call | solution.py:237
  30.9 8.0 %collective-permute-done.1.rest_2_ = bf16[256,256]{1,0:T(8,128)(2,1)S(1)} collective-permute-done((bf16[256,256]{1,0:T(8,128)(2,1)S(1)}, bf16[256,256]{1,0:T(8,128)(2,1)S(1)}, u32[]{:S(2)}, u32[]{:S(2)}) %collective-permute-start.1) | collective-permute-done | bytes 131104 | tf_op jit(solution)/shard_map/ppermute | solution.py:235
  38.9 0.0 copy-start.4
  38.9 2.7 %collective-permute-done.rest_1_ = bf16[256,256]{1,0:T(8,128)(2,1)S(1)} collective-permute-done((bf16[256,256]{1,0:T(8,128)(2,1)S(1)}, bf16[256,256]{1,0:T(8,128)(2,1)S(1)}, u32[]{:S(2)}, u32[]{:S(2)}) %collective-permute-start) | collective-permute-done | bytes 131104 | tf_op jit(solution)/shard_map/ppermute | solution.py:235
  41.6 0.0 copy-done.4
  41.6 0.7 copy-done.5
  42.2 0.0 collective-permute-done.2.rest_3_
  42.2 8.7 %all-to-all-done.1 = bf16[32,64,256]{2,1,0:T(8,128)(2,1)S(1)} async-done(((bf16[32,64,256]{2,1,0:T(8,128)(2,1)}), bf16[32,64,256]{2,1,0:T(8,128)(2,1)S(1)}, u32[]{:S(2)}, u32[]{:S(2)}) %all-to-all-start.1) | async-done | bytes 1048608 | tf_op jit(solution)/shard_map/all_to_all | solution.py:256
  50.9 3.2 %loss.1 = bf16[2048,256]{1,0:T(8,128)(2,1)S(1)} custom-call(f32[1]{0:T(128)S(6)} %copy.11.scale_ref, f32[1]{0:T(128)S(6)} %copy.12.offset_ref, bf16[2048,256]{1,0:T(8,128)(2,1)S(1)} %bitcast.12, bf16[2048,256]{1,0:T(8,128)(2,1)S(1)} %get-tuple-element.9.into_ref, bf16[256,2048]{1,0:T(8,128)(2,1)S(1)} %get-tuple-element.10.out_ref, ...), custom_call_target="tpu_custom_call" | custom-call | flops 30000001024 | bytes 1000000 | tf_op jit(solution)/shard_map/loss/pallas_call | solution.py:258
  54.1 29.6 %all_to_all.22 = bf16[32,64,256]{2,1,0:T(8,128)(2,1)S(1)} all-to-all(bf16[32,64,256]{2,1,0:T(8,128)(2,1)S(1)} %bitcast.13), channel_id=1, replica_groups=mesh['shard'=8,'blk'=4] {'shard','blk'}, dimensions={0} | all-to-all | bytes 2097152 | tf_op jit(solution)/shard_map/all_to_all | solution.py:270
  83.7 0.0 copy-done.1
  83.7 0.0 copy-done.2
  83.7 11.8 %update.1 = (f32[4096,256]{1,0:T(8,128)}, f32[4096,256]{1,0:T(8,128)}) custom-call(s32[32,64]{1,0:T(8,128)S(1)} %bitcast.15, bf16[2048,256]{1,0:T(8,128)(2,1)S(1)} %bitcast.11, f32[4096,256]{1,0:T(8,128)S(1)} %copy-done.1, f32[4096,256]{1,0:T(8,128)S(1)} %copy-done.2), custom_call_target="tpu_custom_call" | custom-call | tf_op jit(solution)/shard_map/update/pallas_call | solution.py:273
  (3 shorter events, 0.0 us)
Async XLA Ops:
  0.6 15.8 %copy-start = (f32[4096,256]{1,0:T(8,128)S(1)}, f32[4096,256]{1,0:T(8,128)}, u32[]{:S(2)}) copy-start(f32[4096,256]{1,0:T(8,128)} %table_ref.3) | copy-start | bytes 12582916
  2.1 22.6 %copy-start.3 = (bf16[256,256]{1,0:T(8,128)(2,1)S(1)}, bf16[256,256]{1,0:T(8,128)(2,1)}, u32[]{:S(2)}) copy-start(bf16[256,256]{1,0:T(8,128)(2,1)} %rest_0_.1) | copy-start | bytes 393220
  22.1 28.8 %all-to-all-start.1 = ((bf16[32,64,256]{2,1,0:T(8,128)(2,1)}), bf16[32,64,256]{2,1,0:T(8,128)(2,1)S(1)}, u32[]{:S(2)}, u32[]{:S(2)}) async-start(bf16[32,64,256]{2,1,0:T(8,128)(2,1)} %bitcast.6), calls=%async_computation.1 | async-start | bytes 2097152 | tf_op jit(solution)/shard_map/all_to_all | solution.py:256
  24.7 14.2 %collective-permute-start.1 = (bf16[256,256]{1,0:T(8,128)(2,1)S(1)}, bf16[256,256]{1,0:T(8,128)(2,1)S(1)}, u32[]{:S(2)}, u32[]{:S(2)}) collective-permute-start(bf16[256,256]{1,0:T(8,128)(2,1)S(1)} %copy-done.3), channel_id=1, source_target_pairs={{0,2},{1,3},{2,0},{3,1},{4,6},{5,7},{6,4},{7,5},{8,10},{9,11},{10,... | collective-permute-start | bytes 393224 | tf_op jit(solution)/shard_map/ppermute | solution.py:235
  26.5 15.1 %collective-permute-start = (bf16[256,256]{1,0:T(8,128)(2,1)S(1)}, bf16[256,256]{1,0:T(8,128)(2,1)S(1)}, u32[]{:S(2)}, u32[]{:S(2)}) collective-permute-start(bf16[256,256]{1,0:T(8,128)(2,1)S(1)} %copy-done.3), channel_id=1, source_target_pairs={{0,1},{1,2},{2,3},{3,0},{4,5},{5,6},{6,7},{7,4},{8,9},{9,10},{10,1... | collective-permute-start | bytes 393224 | tf_op jit(solution)/shard_map/ppermute | solution.py:235
  26.5 15.8 %collective-permute-start.2 = (bf16[256,256]{1,0:T(8,128)(2,1)S(1)}, bf16[256,256]{1,0:T(8,128)(2,1)}, u32[]{:S(2)}, u32[]{:S(2)}) collective-permute-start(bf16[256,256]{1,0:T(8,128)(2,1)S(1)} %copy-done.3), channel_id=1, source_target_pairs={{0,3},{1,0},{2,1},{3,2},{4,7},{5,4},{6,5},{7,6},{8,11},{9,8},{10,9... | collective-permute-start | bytes 393224 | tf_op jit(solution)/shard_map/ppermute | solution.py:235
  38.9 2.7 %copy-start.4 = (bf16[256,256]{1,0:T(8,128)(2,1)}, bf16[256,256]{1,0:T(8,128)(2,1)S(1)}, u32[]{:S(2)}) copy-start(bf16[256,256]{1,0:T(8,128)(2,1)S(1)} %collective-permute-done.1.rest_2_) | copy-start | bytes 393220
  41.6 0.7 copy-start.5
  50.9 32.8 %copy-start.1 = (f32[4096,256]{1,0:T(8,128)S(1)}, f32[4096,256]{1,0:T(8,128)}, u32[]{:S(2)}) copy-start(f32[4096,256]{1,0:T(8,128)} %table_ref.3) | copy-start | bytes 12582916
  50.9 32.8 %copy-start.2 = (f32[4096,256]{1,0:T(8,128)S(1)}, f32[4096,256]{1,0:T(8,128)}, u32[]{:S(2)}) copy-start(f32[4096,256]{1,0:T(8,128)} %energy_ref.1) | copy-start | bytes 12582916

commit v3 on v2

--- a/solution.py
+++ b/solution.py
@@ -72,10 +72,9 @@
         requests_ref[o : o + 1, :] = found[:, o * capacity : (o + 1) * capacity]
 
 
-def prepare_kernel(listed_ref, tally_ref, into_ref, out_ref, share_ref, *, capacity):
+def prepare_kernel(listed_ref, tally_ref, out_ref, share_ref, *, capacity):
     examples = listed_ref.shape[1]
     slots = slot_matrix(listed_ref[...], capacity)
-    into_ref[...] = slots
     same = one_hot(
         lax.broadcasted_iota(I32, (examples, examples), 0)
         == lax.broadcasted_iota(I32, (examples, examples), 1)
@@ -105,24 +104,17 @@
             rows_ref[m : m + step_rows, :] = rows if b == 0 else rows_ref[m : m + step_rows, :] + rows
 
 
-def loss_kernel(scale_ref, offset_ref, answered_ref, into_ref, out_ref, share_ref, *rest):
-    queries, (sent_ref, query_ref, arrived) = rest[:-3], rest[-3:]
+def loss_kernel(scale_ref, offset_ref, answered_ref, listed_ref, out_ref, share_ref, *rest, capacity):
+    queries, sent_ref = rest[:-1], rest[-1]
     examples, width = queries[0].shape
-    loads = [
-        pltpu.make_async_copy(query, query_ref.at[part], arrived.at[part])
-        for part, query in enumerate(queries)
-    ]
-    for load in loads:
-        load.start()
     scale = scale_ref[0]
     offset = offset_ref[0]
     grad_scale = scale / (examples * len(queries))
     share = jnp.concatenate([share_ref[...]] * (width // 128), axis=1)
     items = (dot(out_ref[...], answered_ref[...]) * share).astype(BF16)
     grad = jnp.zeros((examples, width), F32)
-    for part, load in enumerate(loads):
-        load.wait()
-        query = query_ref[part]
+    for part, query_ref in enumerate(queries):
+        query = query_ref[...]
         chance = jax.nn.sigmoid(scale * dot(items, query, NT) + offset)
         if part == 0:
             own = lax.broadcasted_iota(I32, (examples, examples), 0) == lax.broadcasted_iota(
@@ -130,7 +122,8 @@
             )
             chance = chance - jnp.where(own, 1.0, 0.0)
         grad = grad + dot((chance * grad_scale).astype(BF16), query)
-    sent_ref[...] = dot(into_ref[...], (grad * share).astype(BF16)).astype(BF16)
+    slots = slot_matrix(listed_ref[...], capacity)
+    sent_ref[...] = dot(slots, (grad * share).astype(BF16)).astype(BF16)
 
 
 def update_kernel(
@@ -171,14 +164,22 @@
         for store in stores(b, half):
             store.start()
 
-    for b in range(blocks):
-        half = b % 2
-        if b >= 2:
-            for store in stores(b - 2, half):
+    buffers = table_buf.shape[0]
+
+    def turn(b, carry):
+        half = lax.rem(b, buffers)
+
+        @pl.when(b >= buffers)
+        def _():
+            for store in stores(b - buffers, half):
                 store.wait()
+
         step(b, half)
-    for b in (blocks - 2, blocks - 1):
-        for store in stores(b, b % 2):
+        return carry
+
+    lax.fori_loop(0, blocks, turn, 0)
+    for b in range(blocks - buffers, blocks):
+        for store in stores(b, b % buffers):
             store.wait()
 
 
@@ -234,10 +235,9 @@
         queries.append(
             lax.ppermute(query_vectors, "blk", [(b, (b + step) % blocks) for b in range(blocks)])
         )
-    into, out, share = pl.pallas_call(
+    out, share = pl.pallas_call(
         functools.partial(prepare_kernel, capacity=capacity),
         out_shape=(
-            jax.ShapeDtypeStruct((slots, examples), BF16),
             jax.ShapeDtypeStruct((examples, slots), BF16),
             jax.ShapeDtypeStruct((examples, 128), F32),
         ),
@@ -256,17 +256,13 @@
     answered = exchange(fetched.reshape(devices, capacity, width)).reshape(slots, width)
 
     sent = pl.pallas_call(
-        loss_kernel,
-        in_specs=[smem, smem] + [vmem] * 4 + [hbm] * blocks,
+        functools.partial(loss_kernel, capacity=capacity),
+        in_specs=[smem, smem] + [vmem] * (4 + blocks),
         out_shape=jax.ShapeDtypeStruct((slots, width), BF16),
-        scratch_shapes=[
-            pltpu.VMEM((blocks, examples, width), BF16),
-            pltpu.SemaphoreType.DMA((blocks,)),
-        ],
         compiler_params=limit(12),
         cost_estimate=cost(30),
         name="loss",
-    )(score_stretch, offset_term, answered, into, out, share, *map(in_hbm, queries))
+    )(score_stretch, offset_term, answered, listed, out, share, *queries)
     incoming = exchange(sent.reshape(devices, capacity, width)).reshape(slots, width)
 
     block = 512
@@ -280,10 +276,10 @@
         ),
         scratch_shapes=[
             pltpu.VMEM((8, slots), I32),
-            pltpu.VMEM((2, block, width), F32),
-            pltpu.VMEM((2, block, width), F32),
-            pltpu.SemaphoreType.DMA((2,)),
-            pltpu.SemaphoreType.DMA((2,)),
+            pltpu.VMEM((4, block, width), F32),
+            pltpu.VMEM((4, block, width), F32),
+            pltpu.SemaphoreType.DMA((4,)),
+            pltpu.SemaphoreType.DMA((4,)),
         ],
         compiler_params=limit(16),
         name="update",

time: 95.9 us -> 90.5 us (0.944)
  Pallas kernels: 23.5 us -> 18 us
    pallas_call x1, Pallas kernels: 11.8 us -> 7.84 us  [per_device(): pl.pallas_call(update_kernel, in_specs=[vmem] * 4, out_specs=(hbm, hbm),...]
    pallas_call x1, Pallas kernels: 3.19 us -> 1.89 us  [per_device(): pl.pallas_call(functools.partial(loss_kernel, capacity=capacity), in_spec...]
where the time goes in v3:
time: 90.5 us; the launch traced here: 90.2 us
  blocking collectives  43.9 us (49%)
  waiting for transfers between devices  20.3 us (22%)
  Pallas kernels  18 us (20%)
  starting transfers between devices  6.11 us (7%)
  between operations  1.98 us (2%)
    all_to_all x1, blocking collectives, per_device(): exchange(sent.reshape(devices, capacity, width)).reshape(slots, width)  29.6 us
    all_to_all x1, blocking collectives, per_device(): wanted = exchange(requests)  14.3 us
    ppermute x3, waiting for transfers between devices, per_device(): lax.ppermute(query_vectors, 'blk', [(b, (b + step) % blocks) for b in ran...  10.9 us
    all_to_all x1, waiting for transfers between devices, per_device(): exchange(fetched.reshape(devices, capacity, width)).reshape(slots, width)  9.35 us
    pallas_call x1, Pallas kernels, per_device(): pl.pallas_call(update_kernel, in_specs=[vmem] * 4, out_specs=(hbm, hbm),...  7.84 us
    pallas_call x1, Pallas kernels, per_device(): pl.pallas_call(functools.partial(fetch_kernel, step_rows=256, block=1024)...  5.64 us
    ppermute x3, starting transfers between devices, per_device(): lax.ppermute(query_vectors, 'blk', [(b, (b + step) % blocks) for b in ran...  3.46 us
    all_to_all x1, starting transfers between devices, per_device(): exchange(fetched.reshape(devices, capacity, width)).reshape(slots, width)  2.65 us
  transfers between devices with their start and end apart: 4, of which 3 were waited for; matrix products, arithmetic and copies ran while one was open for 0% of the time, Pallas kernels for 1%

profile of v3, /device:TPU:0, one launch (start us, length us, event | category | flops | bytes accessed | tf_op | source)
XLA Modules:
  0.0 90.2 jit_solution(14451079751772610758)
XLA Ops:
  0.6 0.0 copy-start
  0.6 1.5 %route.1 = (s32[32,64]{1,0:T(8,128)S(1)}, s32[32,256]{1,0:T(8,128)S(1)}) custom-call(s32[4,256]{1,0:T(4,128)} %bitcast.19, s32[4,256]{1,0:T(4,128)} %bitcast.20, s32[1,256]{1,0:T(1,128)} %bitcast.17), custom_call_target="tpu_custom_call" | custom-call | flops 10000000000 | bytes 1000000 | tf_op jit(solution)/shard_map/route/pallas_call | solution.py:221
  2.1 0.0 copy-start.3
  2.1 14.3 %all_to_all.21 = s32[32,1,64]{2,1,0:T(1,128)S(1)} all-to-all(s32[32,1,64]{2,1,0:T(1,128)S(1)} %bitcast.16), channel_id=1, replica_groups=mesh['shard'=8,'blk'=4] {'shard','blk'}, dimensions={0} | all-to-all | bytes 16384 | tf_op jit(solution)/shard_map/all_to_all | solution.py:231
  16.4 0.0 copy-done
  16.4 5.6 %fetch.1 = bf16[2048,256]{1,0:T(8,128)(2,1)} custom-call(s32[32,64]{1,0:T(8,128)S(1)} %bitcast.14, f32[4096,256]{1,0:T(8,128)S(1)} %copy-done), custom_call_target="tpu_custom_call" | custom-call | tf_op jit(solution)/shard_map/fetch/pallas_call | solution.py:248
  22.1 2.6 %all-to-all-start.1 = ((bf16[32,64,256]{2,1,0:T(8,128)(2,1)}), bf16[32,64,256]{2,1,0:T(8,128)(2,1)S(1)}, u32[]{:S(2)}, u32[]{:S(2)}) async-start(bf16[32,64,256]{2,1,0:T(8,128)(2,1)} %bitcast.6), calls=%async_computation.1 | async-start | bytes 2097152 | tf_op jit(solution)/shard_map/all_to_all | solution.py:256
  24.7 0.0 copy-done.3
  24.7 1.7 %collective-permute-start.1 = (bf16[256,256]{1,0:T(8,128)(2,1)S(1)}, bf16[256,256]{1,0:T(8,128)(2,1)S(1)}, u32[]{:S(2)}, u32[]{:S(2)}) collective-permute-start(bf16[256,256]{1,0:T(8,128)(2,1)S(1)} %copy-done.3), channel_id=1, source_target_pairs={{0,2},{1,3},{2,0},{3,1},{4,6},{5,7},{6,4},{7,5},{8,10},{9,11},{10,... | collective-permute-start | bytes 393224 | tf_op jit(solution)/shard_map/ppermute | solution.py:236
  26.5 0.0 collective-permute-start
  26.5 1.7 %collective-permute-start.2 = (bf16[256,256]{1,0:T(8,128)(2,1)S(1)}, bf16[256,256]{1,0:T(8,128)(2,1)S(1)}, u32[]{:S(2)}, u32[]{:S(2)}) collective-permute-start(bf16[256,256]{1,0:T(8,128)(2,1)S(1)} %copy-done.3), channel_id=1, source_target_pairs={{0,3},{1,0},{2,1},{3,2},{4,7},{5,4},{6,5},{7,6},{8,11},{9,8},{10,9... | collective-permute-start | bytes 393224 | tf_op jit(solution)/shard_map/ppermute | solution.py:236
  29.5 1.2 %prepare.1 = (bf16[256,2048]{1,0:T(8,128)(2,1)S(1)}, f32[256,128]{1,0:T(8,128)S(1)}) custom-call(s32[32,256]{1,0:T(8,128)S(1)} %get-tuple-element.7.listed_ref, s32[1,256]{1,0:T(1,128)} %bitcast.18), custom_call_target="tpu_custom_call" | custom-call | tf_op jit(solution)/shard_map/prepare/pallas_call | solution.py:238
  30.7 8.2 %collective-permute-done.1.rest_2_ = bf16[256,256]{1,0:T(8,128)(2,1)S(1)} collective-permute-done((bf16[256,256]{1,0:T(8,128)(2,1)S(1)}, bf16[256,256]{1,0:T(8,128)(2,1)S(1)}, u32[]{:S(2)}, u32[]{:S(2)}) %collective-permute-start.1) | collective-permute-done | bytes 131104 | tf_op jit(solution)/shard_map/ppermute | solution.py:236
  38.9 2.7 %collective-permute-done.rest_1_ = bf16[256,256]{1,0:T(8,128)(2,1)S(1)} collective-permute-done((bf16[256,256]{1,0:T(8,128)(2,1)S(1)}, bf16[256,256]{1,0:T(8,128)(2,1)S(1)}, u32[]{:S(2)}, u32[]{:S(2)}) %collective-permute-start) | collective-permute-done | bytes 131104 | tf_op jit(solution)/shard_map/ppermute | solution.py:236
  41.6 0.0 collective-permute-done.2.rest_3_
  41.6 9.4 %all-to-all-done.1 = bf16[32,64,256]{2,1,0:T(8,128)(2,1)S(1)} async-done(((bf16[32,64,256]{2,1,0:T(8,128)(2,1)}), bf16[32,64,256]{2,1,0:T(8,128)(2,1)S(1)}, u32[]{:S(2)}, u32[]{:S(2)}) %all-to-all-start.1) | async-done | bytes 1048608 | tf_op jit(solution)/shard_map/all_to_all | solution.py:256
  50.9 0.0 copy-start.1
  50.9 0.0 copy-start.2
  50.9 1.9 %loss.1 = bf16[2048,256]{1,0:T(8,128)(2,1)S(1)} custom-call(f32[1]{0:T(128)S(6)} %copy.11.scale_ref, f32[1]{0:T(128)S(6)} %copy.12.offset_ref, bf16[2048,256]{1,0:T(8,128)(2,1)S(1)} %bitcast.12, s32[32,256]{1,0:T(8,128)S(1)} %get-tuple-element.7.listed_ref, bf16[256,2048]{1,0:T(8,128)(2,1)S(1)} %get-tuple-element.8.out_ref, ...), custom_call_target="tpu_custom_call" | custom-call | flops 30000001024 | bytes 1000000 | tf_op jit(solution)/shard_map/loss/pallas_call | solution.py:258
  52.8 29.6 %all_to_all.22 = bf16[32,64,256]{2,1,0:T(8,128)(2,1)S(1)} all-to-all(bf16[32,64,256]{2,1,0:T(8,128)(2,1)S(1)} %bitcast.13), channel_id=1, replica_groups=mesh['shard'=8,'blk'=4] {'shard','blk'}, dimensions={0} | all-to-all | bytes 2097152 | tf_op jit(solution)/shard_map/all_to_all | solution.py:266
  82.4 0.0 copy-done.1
  82.4 0.0 copy-done.2
  82.4 7.8 %update.1 = (f32[4096,256]{1,0:T(8,128)}, f32[4096,256]{1,0:T(8,128)}) custom-call(s32[32,64]{1,0:T(8,128)S(1)} %bitcast.15, bf16[2048,256]{1,0:T(8,128)(2,1)S(1)} %bitcast.11, f32[4096,256]{1,0:T(8,128)S(1)} %copy-done.1, f32[4096,256]{1,0:T(8,128)S(1)} %copy-done.2), custom_call_target="tpu_custom_call" | custom-call | tf_op jit(solution)/shard_map/update/pallas_call | solution.py:269
Async XLA Ops:
  0.6 15.8 %copy-start = (f32[4096,256]{1,0:T(8,128)S(1)}, f32[4096,256]{1,0:T(8,128)}, u32[]{:S(2)}) copy-start(f32[4096,256]{1,0:T(8,128)} %table_ref.3) | copy-start | bytes 12582916
  2.1 22.6 %copy-start.3 = (bf16[256,256]{1,0:T(8,128)(2,1)S(1)}, bf16[256,256]{1,0:T(8,128)(2,1)}, u32[]{:S(2)}) copy-start(bf16[256,256]{1,0:T(8,128)(2,1)} %rest_0_.1) | copy-start | bytes 393220
  22.1 28.8 %all-to-all-start.1 = ((bf16[32,64,256]{2,1,0:T(8,128)(2,1)}), bf16[32,64,256]{2,1,0:T(8,128)(2,1)S(1)}, u32[]{:S(2)}, u32[]{:S(2)}) async-start(bf16[32,64,256]{2,1,0:T(8,128)(2,1)} %bitcast.6), calls=%async_computation.1 | async-start | bytes 2097152 | tf_op jit(solution)/shard_map/all_to_all | solution.py:256
  24.7 14.2 %collective-permute-start.1 = (bf16[256,256]{1,0:T(8,128)(2,1)S(1)}, bf16[256,256]{1,0:T(8,128)(2,1)S(1)}, u32[]{:S(2)}, u32[]{:S(2)}) collective-permute-start(bf16[256,256]{1,0:T(8,128)(2,1)S(1)} %copy-done.3), channel_id=1, source_target_pairs={{0,2},{1,3},{2,0},{3,1},{4,6},{5,7},{6,4},{7,5},{8,10},{9,11},{10,... | collective-permute-start | bytes 393224 | tf_op jit(solution)/shard_map/ppermute | solution.py:236
  26.5 15.1 %collective-permute-start = (bf16[256,256]{1,0:T(8,128)(2,1)S(1)}, bf16[256,256]{1,0:T(8,128)(2,1)S(1)}, u32[]{:S(2)}, u32[]{:S(2)}) collective-permute-start(bf16[256,256]{1,0:T(8,128)(2,1)S(1)} %copy-done.3), channel_id=1, source_target_pairs={{0,1},{1,2},{2,3},{3,0},{4,5},{5,6},{6,7},{7,4},{8,9},{9,10},{10,1... | collective-permute-start | bytes 393224 | tf_op jit(solution)/shard_map/ppermute | solution.py:236
  26.5 15.1 %collective-permute-start.2 = (bf16[256,256]{1,0:T(8,128)(2,1)S(1)}, bf16[256,256]{1,0:T(8,128)(2,1)S(1)}, u32[]{:S(2)}, u32[]{:S(2)}) collective-permute-start(bf16[256,256]{1,0:T(8,128)(2,1)S(1)} %copy-done.3), channel_id=1, source_target_pairs={{0,3},{1,0},{2,1},{3,2},{4,7},{5,4},{6,5},{7,6},{8,11},{9,8},{10,9... | collective-permute-start | bytes 393224 | tf_op jit(solution)/shard_map/ppermute | solution.py:236
  50.9 31.5 %copy-start.1 = (f32[4096,256]{1,0:T(8,128)S(1)}, f32[4096,256]{1,0:T(8,128)}, u32[]{:S(2)}) copy-start(f32[4096,256]{1,0:T(8,128)} %table_ref.3) | copy-start | bytes 12582916
  50.9 31.5 %copy-start.2 = (f32[4096,256]{1,0:T(8,128)S(1)}, f32[4096,256]{1,0:T(8,128)}, u32[]{:S(2)}) copy-start(f32[4096,256]{1,0:T(8,128)} %energy_ref.1) | copy-start | bytes 12582916

commit v4 on v3

--- a/solution.py
+++ b/solution.py
@@ -128,59 +128,58 @@
 
 def update_kernel(
     wanted_ref, incoming_ref, table_ref, energy_ref, table_out_ref, energy_out_ref,
-    row_ref, table_buf, energy_buf, table_sem, energy_sem,
+    row_ref, table_buf, energy_buf, sent, *, chunk, depth, piece,
 ):
     devices, capacity = wanted_ref.shape
     slots, _ = incoming_ref.shape
-    block = table_buf.shape[1]
-    blocks = table_ref.shape[0] // block
+    rows = table_ref.shape[0]
     for s in range(devices):
         row_ref[:, s * capacity : (s + 1) * capacity] = jnp.broadcast_to(
             wanted_ref[s : s + 1, :], (8, capacity)
         )
-    place = lax.broadcasted_iota(I32, (block, 128), 0)
-
-    def stores(b, half):
-        at = pl.ds(pl.multiple_of(b * block, block), block)
+
+    def stores(at):
         return (
-            pltpu.make_async_copy(table_buf.at[half], table_out_ref.at[at, :], table_sem.at[half]),
-            pltpu.make_async_copy(energy_buf.at[half], energy_out_ref.at[at, :], energy_sem.at[half]),
-        )
-
-    def step(b, half):
-        at = pl.ds(pl.multiple_of(b * block, block), block)
-        here = place + b * block
-        hot = jnp.concatenate(
-            [
-                one_hot(jnp.broadcast_to(row_ref[0:1, c : c + 128], (block, 128)) == here)
-                for c in range(0, slots, 128)
-            ],
-            axis=1,
-        )
-        grad = dot(hot, incoming_ref[...])
+            pltpu.make_async_copy(table_buf.at[at, :], table_out_ref.at[at, :], sent.at[0]),
+            pltpu.make_async_copy(energy_buf.at[at, :], energy_out_ref.at[at, :], sent.at[1]),
+        )
+
+    def row_grad(base):
+        here = lax.broadcasted_iota(I32, (chunk, 128), 0) + base
+        total = None
+        for k in range(0, slots, depth):
+            hot = jnp.concatenate(
+                [
+                    one_hot(jnp.broadcast_to(row_ref[0:1, c : c + 128], (chunk, 128)) == here)
+                    for c in range(k, k + depth, 128)
+                ],
+                axis=1,
+            )
+            part = dot(hot, incoming_ref[k : k + depth, :])
+            total = part if total is None else total + part
+        return total
+
+    def adagrad(base, grad):
+        at = pl.ds(pl.multiple_of(base, chunk), chunk)
         energy = energy_ref[at, :] + grad * grad
-        energy_buf[half] = energy
-        table_buf[half] = table_ref[at, :] - LEARN_RATE * grad / (jnp.sqrt(energy) + ADAGRAD_EPSILON)
-        for store in stores(b, half):
-            store.start()
-
-    buffers = table_buf.shape[0]
-
-    def turn(b, carry):
-        half = lax.rem(b, buffers)
-
-        @pl.when(b >= buffers)
-        def _():
-            for store in stores(b - buffers, half):
-                store.wait()
-
-        step(b, half)
+        energy_buf[at, :] = energy
+        table_buf[at, :] = table_ref[at, :] - LEARN_RATE * grad / (jnp.sqrt(energy) + ADAGRAD_EPSILON)
+
+    def sweep(i, carry):
+        first = i * rows
+        grad = row_grad(first)
+        for q in range(chunk, rows + chunk, chunk):
+            after = row_grad(first + q) if q < rows else None
+            adagrad(first + q - chunk, grad)
+            grad = after
+            if q % piece == 0:
+                for store in stores(pl.ds(pl.multiple_of(first + q - piece, piece), piece)):
+                    store.start()
         return carry
 
-    lax.fori_loop(0, blocks, turn, 0)
-    for b in range(blocks - buffers, blocks):
-        for store in stores(b, b % buffers):
-            store.wait()
+    lax.fori_loop(0, 1, sweep, 0)
+    for store in stores(pl.ds(0, rows)):
+        store.wait()
 
 
 def per_device(
@@ -265,9 +264,8 @@
     )(score_stretch, offset_term, answered, listed, out, share, *queries)
     incoming = exchange(sent.reshape(devices, capacity, width)).reshape(slots, width)
 
-    block = 512
     return pl.pallas_call(
-        update_kernel,
+        functools.partial(update_kernel, chunk=256, depth=1024, piece=512),
         in_specs=[vmem] * 4,
         out_specs=(hbm, hbm),
         out_shape=(
@@ -276,12 +274,11 @@
         ),
         scratch_shapes=[
             pltpu.VMEM((8, slots), I32),
-            pltpu.VMEM((4, block, width), F32),
-            pltpu.VMEM((4, block, width), F32),
-            pltpu.SemaphoreType.DMA((4,)),
-            pltpu.SemaphoreType.DMA((4,)),
+            pltpu.VMEM((table_rows, width), F32),
+            pltpu.VMEM((table_rows, width), F32),
+            pltpu.SemaphoreType.DMA((2,)),
         ],
-        compiler_params=limit(16),
+        compiler_params=limit(24),
         name="update",
     )(wanted, incoming, item_embedding_matrix, running_grad_energy)
 

time: 90.5 us -> 89.8 us (level)
  no operation moved by 1% of the time
where the time goes in v4:
time: 89.8 us; the launch traced here: 89.5 us
  blocking collectives  43.9 us (49%)
  waiting for transfers between devices  20.2 us (22%)
  Pallas kernels  17.2 us (19%)
  starting transfers between devices  6.11 us (7%)
  between operations  2.14 us (2%)
    all_to_all x1, blocking collectives, per_device(): exchange(sent.reshape(devices, capacity, width)).reshape(slots, width)  29.6 us
    all_to_all x1, blocking collectives, per_device(): wanted = exchange(requests)  14.3 us
    ppermute x3, waiting for transfers between devices, per_device(): lax.ppermute(query_vectors, 'blk', [(b, (b + step) % blocks) for b in ran...  10.9 us
    all_to_all x1, waiting for transfers between devices, per_device(): exchange(fetched.reshape(devices, capacity, width)).reshape(slots, width)  9.35 us
    pallas_call x1, Pallas kernels, per_device(): pl.pallas_call(functools.partial(update_kernel, chunk=256, depth=1024, pi...  7 us
    pallas_call x1, Pallas kernels, per_device(): pl.pallas_call(functools.partial(fetch_kernel, step_rows=256, block=1024)...  5.64 us
    ppermute x3, starting transfers between devices, per_device(): lax.ppermute(query_vectors, 'blk', [(b, (b + step) % blocks) for b in ran...  3.46 us
    all_to_all x1, starting transfers between devices, per_device(): exchange(fetched.reshape(devices, capacity, width)).reshape(slots, width)  2.65 us
  transfers between devices with their start and end apart: 4, of which 3 were waited for; matrix products, arithmetic and copies ran while one was open for 0% of the time, Pallas kernels for 1%

profile of v4, /device:TPU:0, one launch (start us, length us, event | category | flops | bytes accessed | tf_op | source)
XLA Modules:
  0.0 89.5 jit_solution(11276604136983772407)
XLA Ops:
  0.6 0.0 copy-start
  0.6 1.5 %route.1 = (s32[32,64]{1,0:T(8,128)S(1)}, s32[32,256]{1,0:T(8,128)S(1)}) custom-call(s32[4,256]{1,0:T(4,128)} %bitcast.19, s32[4,256]{1,0:T(4,128)} %bitcast.20, s32[1,256]{1,0:T(1,128)} %bitcast.17), custom_call_target="tpu_custom_call" | custom-call | flops 10000000000 | bytes 1000000 | tf_op jit(solution)/shard_map/route/pallas_call | solution.py:220
  2.1 0.0 copy-start.3
  2.1 14.3 %all_to_all.21 = s32[32,1,64]{2,1,0:T(1,128)S(1)} all-to-all(s32[32,1,64]{2,1,0:T(1,128)S(1)} %bitcast.16), channel_id=1, replica_groups=mesh['shard'=8,'blk'=4] {'shard','blk'}, dimensions={0} | all-to-all | bytes 16384 | tf_op jit(solution)/shard_map/all_to_all | solution.py:230
  16.4 0.0 copy-done
  16.4 5.6 %fetch.1 = bf16[2048,256]{1,0:T(8,128)(2,1)} custom-call(s32[32,64]{1,0:T(8,128)S(1)} %bitcast.14, f32[4096,256]{1,0:T(8,128)S(1)} %copy-done), custom_call_target="tpu_custom_call" | custom-call | tf_op jit(solution)/shard_map/fetch/pallas_call | solution.py:247
  22.1 2.6 %all-to-all-start.1 = ((bf16[32,64,256]{2,1,0:T(8,128)(2,1)}), bf16[32,64,256]{2,1,0:T(8,128)(2,1)S(1)}, u32[]{:S(2)}, u32[]{:S(2)}) async-start(bf16[32,64,256]{2,1,0:T(8,128)(2,1)} %bitcast.6), calls=%async_computation.1 | async-start | bytes 2097152 | tf_op jit(solution)/shard_map/all_to_all | solution.py:255
  24.7 0.0 copy-done.3
  24.7 1.7 %collective-permute-start.1 = (bf16[256,256]{1,0:T(8,128)(2,1)S(1)}, bf16[256,256]{1,0:T(8,128)(2,1)S(1)}, u32[]{:S(2)}, u32[]{:S(2)}) collective-permute-start(bf16[256,256]{1,0:T(8,128)(2,1)S(1)} %copy-done.3), channel_id=1, source_target_pairs={{0,2},{1,3},{2,0},{3,1},{4,6},{5,7},{6,4},{7,5},{8,10},{9,11},{10,... | collective-permute-start | bytes 393224 | tf_op jit(solution)/shard_map/ppermute | solution.py:235
  26.5 0.0 collective-permute-start
  26.5 1.7 %collective-permute-start.2 = (bf16[256,256]{1,0:T(8,128)(2,1)S(1)}, bf16[256,256]{1,0:T(8,128)(2,1)S(1)}, u32[]{:S(2)}, u32[]{:S(2)}) collective-permute-start(bf16[256,256]{1,0:T(8,128)(2,1)S(1)} %copy-done.3), channel_id=1, source_target_pairs={{0,3},{1,0},{2,1},{3,2},{4,7},{5,4},{6,5},{7,6},{8,11},{9,8},{10,9... | collective-permute-start | bytes 393224 | tf_op jit(solution)/shard_map/ppermute | solution.py:235
  29.5 1.2 %prepare.1 = (bf16[256,2048]{1,0:T(8,128)(2,1)S(1)}, f32[256,128]{1,0:T(8,128)S(1)}) custom-call(s32[32,256]{1,0:T(8,128)S(1)} %get-tuple-element.7.listed_ref, s32[1,256]{1,0:T(1,128)} %bitcast.18), custom_call_target="tpu_custom_call" | custom-call | tf_op jit(solution)/shard_map/prepare/pallas_call | solution.py:237
  30.7 8.2 %collective-permute-done.1.rest_2_ = bf16[256,256]{1,0:T(8,128)(2,1)S(1)} collective-permute-done((bf16[256,256]{1,0:T(8,128)(2,1)S(1)}, bf16[256,256]{1,0:T(8,128)(2,1)S(1)}, u32[]{:S(2)}, u32[]{:S(2)}) %collective-permute-start.1) | collective-permute-done | bytes 131104 | tf_op jit(solution)/shard_map/ppermute | solution.py:235
  38.9 2.7 %collective-permute-done.rest_1_ = bf16[256,256]{1,0:T(8,128)(2,1)S(1)} collective-permute-done((bf16[256,256]{1,0:T(8,128)(2,1)S(1)}, bf16[256,256]{1,0:T(8,128)(2,1)S(1)}, u32[]{:S(2)}, u32[]{:S(2)}) %collective-permute-start) | collective-permute-done | bytes 131104 | tf_op jit(solution)/shard_map/ppermute | solution.py:235
  41.6 0.0 collective-permute-done.2.rest_3_
  41.6 9.4 %all-to-all-done.1 = bf16[32,64,256]{2,1,0:T(8,128)(2,1)S(1)} async-done(((bf16[32,64,256]{2,1,0:T(8,128)(2,1)}), bf16[32,64,256]{2,1,0:T(8,128)(2,1)S(1)}, u32[]{:S(2)}, u32[]{:S(2)}) %all-to-all-start.1) | async-done | bytes 1048608 | tf_op jit(solution)/shard_map/all_to_all | solution.py:255
  50.9 0.0 copy-start.1
  50.9 0.0 copy-start.2
  50.9 1.9 %loss.1 = bf16[2048,256]{1,0:T(8,128)(2,1)S(1)} custom-call(f32[1]{0:T(128)S(6)} %copy.11.scale_ref, f32[1]{0:T(128)S(6)} %copy.12.offset_ref, bf16[2048,256]{1,0:T(8,128)(2,1)S(1)} %bitcast.12, s32[32,256]{1,0:T(8,128)S(1)} %get-tuple-element.7.listed_ref, bf16[256,2048]{1,0:T(8,128)(2,1)S(1)} %get-tuple-element.8.out_ref, ...), custom_call_target="tpu_custom_call" | custom-call | flops 30000001024 | bytes 1000000 | tf_op jit(solution)/shard_map/loss/pallas_call | solution.py:257
  52.8 29.6 %all_to_all.22 = bf16[32,64,256]{2,1,0:T(8,128)(2,1)S(1)} all-to-all(bf16[32,64,256]{2,1,0:T(8,128)(2,1)S(1)} %bitcast.13), channel_id=1, replica_groups=mesh['shard'=8,'blk'=4] {'shard','blk'}, dimensions={0} | all-to-all | bytes 2097152 | tf_op jit(solution)/shard_map/all_to_all | solution.py:265
  82.4 0.0 copy-done.1
  82.4 0.0 copy-done.2
  82.4 7.0 %update.1 = (f32[4096,256]{1,0:T(8,128)}, f32[4096,256]{1,0:T(8,128)}) custom-call(s32[32,64]{1,0:T(8,128)S(1)} %bitcast.15, bf16[2048,256]{1,0:T(8,128)(2,1)S(1)} %bitcast.11, f32[4096,256]{1,0:T(8,128)S(1)} %copy-done.1, f32[4096,256]{1,0:T(8,128)S(1)} %copy-done.2), custom_call_target="tpu_custom_call" | custom-call | tf_op jit(solution)/shard_map/update/pallas_call | solution.py:267
Async XLA Ops:
  0.6 15.8 %copy-start = (f32[4096,256]{1,0:T(8,128)S(1)}, f32[4096,256]{1,0:T(8,128)}, u32[]{:S(2)}) copy-start(f32[4096,256]{1,0:T(8,128)} %table_ref.3) | copy-start | bytes 12582916
  2.1 22.6 %copy-start.3 = (bf16[256,256]{1,0:T(8,128)(2,1)S(1)}, bf16[256,256]{1,0:T(8,128)(2,1)}, u32[]{:S(2)}) copy-start(bf16[256,256]{1,0:T(8,128)(2,1)} %rest_0_.1) | copy-start | bytes 393220
  22.1 28.8 %all-to-all-start.1 = ((bf16[32,64,256]{2,1,0:T(8,128)(2,1)}), bf16[32,64,256]{2,1,0:T(8,128)(2,1)S(1)}, u32[]{:S(2)}, u32[]{:S(2)}) async-start(bf16[32,64,256]{2,1,0:T(8,128)(2,1)} %bitcast.6), calls=%async_computation.1 | async-start | bytes 2097152 | tf_op jit(solution)/shard_map/all_to_all | solution.py:255
  24.7 14.2 %collective-permute-start.1 = (bf16[256,256]{1,0:T(8,128)(2,1)S(1)}, bf16[256,256]{1,0:T(8,128)(2,1)S(1)}, u32[]{:S(2)}, u32[]{:S(2)}) collective-permute-start(bf16[256,256]{1,0:T(8,128)(2,1)S(1)} %copy-done.3), channel_id=1, source_target_pairs={{0,2},{1,3},{2,0},{3,1},{4,6},{5,7},{6,4},{7,5},{8,10},{9,11},{10,... | collective-permute-start | bytes 393224 | tf_op jit(solution)/shard_map/ppermute | solution.py:235
  26.5 15.1 %collective-permute-start = (bf16[256,256]{1,0:T(8,128)(2,1)S(1)}, bf16[256,256]{1,0:T(8,128)(2,1)S(1)}, u32[]{:S(2)}, u32[]{:S(2)}) collective-permute-start(bf16[256,256]{1,0:T(8,128)(2,1)S(1)} %copy-done.3), channel_id=1, source_target_pairs={{0,1},{1,2},{2,3},{3,0},{4,5},{5,6},{6,7},{7,4},{8,9},{9,10},{10,1... | collective-permute-start | bytes 393224 | tf_op jit(solution)/shard_map/ppermute | solution.py:235
  26.5 15.1 %collective-permute-start.2 = (bf16[256,256]{1,0:T(8,128)(2,1)S(1)}, bf16[256,256]{1,0:T(8,128)(2,1)S(1)}, u32[]{:S(2)}, u32[]{:S(2)}) collective-permute-start(bf16[256,256]{1,0:T(8,128)(2,1)S(1)} %copy-done.3), channel_id=1, source_target_pairs={{0,3},{1,0},{2,1},{3,2},{4,7},{5,4},{6,5},{7,6},{8,11},{9,8},{10,9... | collective-permute-start | bytes 393224 | tf_op jit(solution)/shard_map/ppermute | solution.py:235
  50.9 31.5 %copy-start.1 = (f32[4096,256]{1,0:T(8,128)S(1)}, f32[4096,256]{1,0:T(8,128)}, u32[]{:S(2)}) copy-start(f32[4096,256]{1,0:T(8,128)} %table_ref.3) | copy-start | bytes 12582916
  50.9 31.5 %copy-start.2 = (f32[4096,256]{1,0:T(8,128)S(1)}, f32[4096,256]{1,0:T(8,128)}, u32[]{:S(2)}) copy-start(f32[4096,256]{1,0:T(8,128)} %energy_ref.1) | copy-start | bytes 12582916

commit v5 on v4

--- a/solution.py
+++ b/solution.py
@@ -265,7 +265,7 @@
     incoming = exchange(sent.reshape(devices, capacity, width)).reshape(slots, width)
 
     return pl.pallas_call(
-        functools.partial(update_kernel, chunk=256, depth=1024, piece=512),
+        functools.partial(update_kernel, chunk=256, depth=1024, piece=256),
         in_specs=[vmem] * 4,
         out_specs=(hbm, hbm),
         out_shape=(

time: 89.8 us -> 90.2 us (level)
  no operation moved by 1% of the time
where the time goes in v5:
time: 90.2 us; the launch traced here: 89.9 us
  blocking collectives  43.9 us (49%)
  waiting for transfers between devices  20.2 us (22%)
  Pallas kernels  17.5 us (19%)
  starting transfers between devices  6.11 us (7%)
  between operations  2.14 us (2%)
    all_to_all x1, blocking collectives, per_device(): exchange(sent.reshape(devices, capacity, width)).reshape(slots, width)  29.6 us
    all_to_all x1, blocking collectives, per_device(): wanted = exchange(requests)  14.3 us
    ppermute x3, waiting for transfers between devices, per_device(): lax.ppermute(query_vectors, 'blk', [(b, (b + step) % blocks) for b in ran...  10.9 us
    all_to_all x1, waiting for transfers between devices, per_device(): exchange(fetched.reshape(devices, capacity, width)).reshape(slots, width)  9.35 us
    pallas_call x1, Pallas kernels, per_device(): pl.pallas_call(functools.partial(update_kernel, chunk=256, depth=1024, pi...  7.38 us
    pallas_call x1, Pallas kernels, per_device(): pl.pallas_call(functools.partial(fetch_kernel, step_rows=256, block=1024)...  5.64 us
    ppermute x3, starting transfers between devices, per_device(): lax.ppermute(query_vectors, 'blk', [(b, (b + step) % blocks) for b in ran...  3.46 us
    all_to_all x1, starting transfers between devices, per_device(): exchange(fetched.reshape(devices, capacity, width)).reshape(slots, width)  2.65 us
  transfers between devices with their start and end apart: 4, of which 3 were waited for; matrix products, arithmetic and copies ran while one was open for 0% of the time, Pallas kernels for 1%

profile of v5, /device:TPU:0, one launch (start us, length us, event | category | flops | bytes accessed | tf_op | source)
XLA Modules:
  0.0 89.9 jit_solution(5182284470501225121)
XLA Ops:
  0.6 0.0 copy-start
  0.6 1.5 %route.1 = (s32[32,64]{1,0:T(8,128)S(1)}, s32[32,256]{1,0:T(8,128)S(1)}) custom-call(s32[4,256]{1,0:T(4,128)} %bitcast.19, s32[4,256]{1,0:T(4,128)} %bitcast.20, s32[1,256]{1,0:T(1,128)} %bitcast.17), custom_call_target="tpu_custom_call" | custom-call | flops 10000000000 | bytes 1000000 | tf_op jit(solution)/shard_map/route/pallas_call | solution.py:220
  2.1 0.0 copy-start.3
  2.1 14.3 %all_to_all.21 = s32[32,1,64]{2,1,0:T(1,128)S(1)} all-to-all(s32[32,1,64]{2,1,0:T(1,128)S(1)} %bitcast.16), channel_id=1, replica_groups=mesh['shard'=8,'blk'=4] {'shard','blk'}, dimensions={0} | all-to-all | bytes 16384 | tf_op jit(solution)/shard_map/all_to_all | solution.py:230
  16.4 0.0 copy-done
  16.4 5.6 %fetch.1 = bf16[2048,256]{1,0:T(8,128)(2,1)} custom-call(s32[32,64]{1,0:T(8,128)S(1)} %bitcast.14, f32[4096,256]{1,0:T(8,128)S(1)} %copy-done), custom_call_target="tpu_custom_call" | custom-call | tf_op jit(solution)/shard_map/fetch/pallas_call | solution.py:247
  22.1 2.6 %all-to-all-start.1 = ((bf16[32,64,256]{2,1,0:T(8,128)(2,1)}), bf16[32,64,256]{2,1,0:T(8,128)(2,1)S(1)}, u32[]{:S(2)}, u32[]{:S(2)}) async-start(bf16[32,64,256]{2,1,0:T(8,128)(2,1)} %bitcast.6), calls=%async_computation.1 | async-start | bytes 2097152 | tf_op jit(solution)/shard_map/all_to_all | solution.py:255
  24.7 0.0 copy-done.3
  24.7 1.7 %collective-permute-start.1 = (bf16[256,256]{1,0:T(8,128)(2,1)S(1)}, bf16[256,256]{1,0:T(8,128)(2,1)S(1)}, u32[]{:S(2)}, u32[]{:S(2)}) collective-permute-start(bf16[256,256]{1,0:T(8,128)(2,1)S(1)} %copy-done.3), channel_id=1, source_target_pairs={{0,2},{1,3},{2,0},{3,1},{4,6},{5,7},{6,4},{7,5},{8,10},{9,11},{10,... | collective-permute-start | bytes 393224 | tf_op jit(solution)/shard_map/ppermute | solution.py:235
  26.5 0.0 collective-permute-start
  26.5 1.7 %collective-permute-start.2 = (bf16[256,256]{1,0:T(8,128)(2,1)S(1)}, bf16[256,256]{1,0:T(8,128)(2,1)S(1)}, u32[]{:S(2)}, u32[]{:S(2)}) collective-permute-start(bf16[256,256]{1,0:T(8,128)(2,1)S(1)} %copy-done.3), channel_id=1, source_target_pairs={{0,3},{1,0},{2,1},{3,2},{4,7},{5,4},{6,5},{7,6},{8,11},{9,8},{10,9... | collective-permute-start | bytes 393224 | tf_op jit(solution)/shard_map/ppermute | solution.py:235
  29.5 1.2 %prepare.1 = (bf16[256,2048]{1,0:T(8,128)(2,1)S(1)}, f32[256,128]{1,0:T(8,128)S(1)}) custom-call(s32[32,256]{1,0:T(8,128)S(1)} %get-tuple-element.7.listed_ref, s32[1,256]{1,0:T(1,128)} %bitcast.18), custom_call_target="tpu_custom_call" | custom-call | tf_op jit(solution)/shard_map/prepare/pallas_call | solution.py:237
  30.7 8.2 %collective-permute-done.1.rest_2_ = bf16[256,256]{1,0:T(8,128)(2,1)S(1)} collective-permute-done((bf16[256,256]{1,0:T(8,128)(2,1)S(1)}, bf16[256,256]{1,0:T(8,128)(2,1)S(1)}, u32[]{:S(2)}, u32[]{:S(2)}) %collective-permute-start.1) | collective-permute-done | bytes 131104 | tf_op jit(solution)/shard_map/ppermute | solution.py:235
  38.9 2.7 %collective-permute-done.rest_1_ = bf16[256,256]{1,0:T(8,128)(2,1)S(1)} collective-permute-done((bf16[256,256]{1,0:T(8,128)(2,1)S(1)}, bf16[256,256]{1,0:T(8,128)(2,1)S(1)}, u32[]{:S(2)}, u32[]{:S(2)}) %collective-permute-start) | collective-permute-done | bytes 131104 | tf_op jit(solution)/shard_map/ppermute | solution.py:235
  41.6 0.0 collective-permute-done.2.rest_3_
  41.6 9.4 %all-to-all-done.1 = bf16[32,64,256]{2,1,0:T(8,128)(2,1)S(1)} async-done(((bf16[32,64,256]{2,1,0:T(8,128)(2,1)}), bf16[32,64,256]{2,1,0:T(8,128)(2,1)S(1)}, u32[]{:S(2)}, u32[]{:S(2)}) %all-to-all-start.1) | async-done | bytes 1048608 | tf_op jit(solution)/shard_map/all_to_all | solution.py:255
  50.9 0.0 copy-start.1
  50.9 0.0 copy-start.2
  50.9 1.9 %loss.1 = bf16[2048,256]{1,0:T(8,128)(2,1)S(1)} custom-call(f32[1]{0:T(128)S(6)} %copy.11.scale_ref, f32[1]{0:T(128)S(6)} %copy.12.offset_ref, bf16[2048,256]{1,0:T(8,128)(2,1)S(1)} %bitcast.12, s32[32,256]{1,0:T(8,128)S(1)} %get-tuple-element.7.listed_ref, bf16[256,2048]{1,0:T(8,128)(2,1)S(1)} %get-tuple-element.8.out_ref, ...), custom_call_target="tpu_custom_call" | custom-call | flops 30000001024 | bytes 1000000 | tf_op jit(solution)/shard_map/loss/pallas_call | solution.py:257
  52.8 29.6 %all_to_all.22 = bf16[32,64,256]{2,1,0:T(8,128)(2,1)S(1)} all-to-all(bf16[32,64,256]{2,1,0:T(8,128)(2,1)S(1)} %bitcast.13), channel_id=1, replica_groups=mesh['shard'=8,'blk'=4] {'shard','blk'}, dimensions={0} | all-to-all | bytes 2097152 | tf_op jit(solution)/shard_map/all_to_all | solution.py:265
  82.4 0.0 copy-done.1
  82.4 0.0 copy-done.2
  82.4 7.4 %update.1 = (f32[4096,256]{1,0:T(8,128)}, f32[4096,256]{1,0:T(8,128)}) custom-call(s32[32,64]{1,0:T(8,128)S(1)} %bitcast.15, bf16[2048,256]{1,0:T(8,128)(2,1)S(1)} %bitcast.11, f32[4096,256]{1,0:T(8,128)S(1)} %copy-done.1, f32[4096,256]{1,0:T(8,128)S(1)} %copy-done.2), custom_call_target="tpu_custom_call" | custom-call | tf_op jit(solution)/shard_map/update/pallas_call | solution.py:267
Async XLA Ops:
  0.6 15.8 %copy-start = (f32[4096,256]{1,0:T(8,128)S(1)}, f32[4096,256]{1,0:T(8,128)}, u32[]{:S(2)}) copy-start(f32[4096,256]{1,0:T(8,128)} %table_ref.3) | copy-start | bytes 12582916
  2.1 22.6 %copy-start.3 = (bf16[256,256]{1,0:T(8,128)(2,1)S(1)}, bf16[256,256]{1,0:T(8,128)(2,1)}, u32[]{:S(2)}) copy-start(bf16[256,256]{1,0:T(8,128)(2,1)} %rest_0_.1) | copy-start | bytes 393220
  22.1 28.8 %all-to-all-start.1 = ((bf16[32,64,256]{2,1,0:T(8,128)(2,1)}), bf16[32,64,256]{2,1,0:T(8,128)(2,1)S(1)}, u32[]{:S(2)}, u32[]{:S(2)}) async-start(bf16[32,64,256]{2,1,0:T(8,128)(2,1)} %bitcast.6), calls=%async_computation.1 | async-start | bytes 2097152 | tf_op jit(solution)/shard_map/all_to_all | solution.py:255
  24.7 14.2 %collective-permute-start.1 = (bf16[256,256]{1,0:T(8,128)(2,1)S(1)}, bf16[256,256]{1,0:T(8,128)(2,1)S(1)}, u32[]{:S(2)}, u32[]{:S(2)}) collective-permute-start(bf16[256,256]{1,0:T(8,128)(2,1)S(1)} %copy-done.3), channel_id=1, source_target_pairs={{0,2},{1,3},{2,0},{3,1},{4,6},{5,7},{6,4},{7,5},{8,10},{9,11},{10,... | collective-permute-start | bytes 393224 | tf_op jit(solution)/shard_map/ppermute | solution.py:235
  26.5 15.1 %collective-permute-start = (bf16[256,256]{1,0:T(8,128)(2,1)S(1)}, bf16[256,256]{1,0:T(8,128)(2,1)S(1)}, u32[]{:S(2)}, u32[]{:S(2)}) collective-permute-start(bf16[256,256]{1,0:T(8,128)(2,1)S(1)} %copy-done.3), channel_id=1, source_target_pairs={{0,1},{1,2},{2,3},{3,0},{4,5},{5,6},{6,7},{7,4},{8,9},{9,10},{10,1... | collective-permute-start | bytes 393224 | tf_op jit(solution)/shard_map/ppermute | solution.py:235
  26.5 15.1 %collective-permute-start.2 = (bf16[256,256]{1,0:T(8,128)(2,1)S(1)}, bf16[256,256]{1,0:T(8,128)(2,1)S(1)}, u32[]{:S(2)}, u32[]{:S(2)}) collective-permute-start(bf16[256,256]{1,0:T(8,128)(2,1)S(1)} %copy-done.3), channel_id=1, source_target_pairs={{0,3},{1,0},{2,1},{3,2},{4,7},{5,4},{6,5},{7,6},{8,11},{9,8},{10,9... | collective-permute-start | bytes 393224 | tf_op jit(solution)/shard_map/ppermute | solution.py:235
  50.9 31.5 %copy-start.1 = (f32[4096,256]{1,0:T(8,128)S(1)}, f32[4096,256]{1,0:T(8,128)}, u32[]{:S(2)}) copy-start(f32[4096,256]{1,0:T(8,128)} %table_ref.3) | copy-start | bytes 12582916
  50.9 31.5 %copy-start.2 = (f32[4096,256]{1,0:T(8,128)S(1)}, f32[4096,256]{1,0:T(8,128)}, u32[]{:S(2)}) copy-start(f32[4096,256]{1,0:T(8,128)} %energy_ref.1) | copy-start | bytes 12582916
